TPU v7x, 256 devices: a whole 4x4x8 slice. The times are simulated.
256 devices in a mesh: px: 4 (over y_lo, core), py: 8 (over x, y_hi), dom: 8 (over z).
Axes of the slice: x: 4, y: 4 (y_hi: 2, y_lo: 2; y = y_hi * 2 + y_lo), z: 8, core: 2. Of those that a mesh axis runs over, the one named last changes fastest.
Arguments:
- velocity: float32 [16, 64, 256, 128], P('dom', 'px', 'py'), may hold values from 0.65 to 2.2
- buoyancy: float32 [64, 256, 128], P('px', 'py'), may hold values from 0.6 to 1.6
- forward_prev: float32 [16, 64, 256, 128], P('dom', 'px', 'py'), may hold values from -12 to 12
- forward_now: float32 [16, 64, 256, 128], P('dom', 'px', 'py'), may hold values from -12 to 12
- adjoint_prev: float32 [16, 64, 256, 128], P('dom', 'px', 'py'), may hold values from -12 to 12
- adjoint_now: float32 [16, 64, 256, 128], P('dom', 'px', 'py'), may hold values from -12 to 12
- sources: int32 [16], P('dom'), may hold values from 0 to 2097151
- wavelet: float32 [16, 3], P('dom'), may hold values from -800 to 800
- receivers: int32 [16, 1024], P('dom'), may hold values from 0 to 2097151
- misfit: float32 [16, 3, 1024], P('dom'), may hold values from -6 to 6
- sponge: int32 [6], replicated, may hold values from 2 to 8
Outputs:
- forward_before: float32 [16, 64, 256, 128], P('dom', 'px', 'py')
- forward_after: float32 [16, 64, 256, 128], P('dom', 'px', 'py')
- adjoint_before: float32 [16, 64, 256, 128], P('dom', 'px', 'py')
- adjoint_after: float32 [16, 64, 256, 128], P('dom', 'px', 'py')
- drift: float32 [16, 64, 256, 128], P('dom', 'px', 'py')
- spread: float32 [16, 64, 256, 128], P('dom', 'px', 'py')
All inputs are finite; a program needn't handle non-finite values.
Results may differ from a plain program's by a relative error of at most 0.0003.
Values sent between devices are 32-bit elements; how exact they have to be, the bound alone decides.
A program may use at most 64 MiB of HBM per device.

v0:
```python
import jax
import jax.numpy as jnp
from jax import lax
from jax.sharding import PartitionSpec as P

EPSILON = 1e-06
TIME_STEP = 0.18
SPONGE_RATE = 0.5
NEAR_WEIGHT = 9.0 / 8.0
FAR_WEIGHT = 1.0 / 24.0


def with_halo(cells, sides, width):
    for axis, dim in sides:
        count = lax.axis_size(axis)
        ends = count - 1
        head = lax.slice_in_dim(cells, 0, width, axis=dim)
        tail = lax.slice_in_dim(cells, cells.shape[dim] - width, cells.shape[dim], axis=dim)
        cells = jnp.concatenate(
            [
                lax.ppermute(tail, axis, [(i, (i + 1) % count) for i in range(ends)]),
                cells,
                lax.ppermute(head, axis, [((i + 1) % count, i) for i in range(ends)]),
            ],
            axis=dim,
        )
    return cells


def take_slab(source_array, start_at, amount, which_axis):
    return lax.slice_in_dim(
        source_array, start_at, start_at + amount, axis=source_array.ndim + which_axis
    )


def axis_term(wave_field, buoy_field, extent, which_axis):
    half_buoy = 0.5 * (
        take_slab(buoy_field, 1, extent + 3, which_axis)
        + take_slab(buoy_field, 2, extent + 3, which_axis)
    )
    slope_face = NEAR_WEIGHT * (
        take_slab(wave_field, 2, extent + 3, which_axis)
        - take_slab(wave_field, 1, extent + 3, which_axis)
    ) - FAR_WEIGHT * (
        take_slab(wave_field, 3, extent + 3, which_axis)
        - take_slab(wave_field, 0, extent + 3, which_axis)
    )
    flux_face = half_buoy * slope_face
    return NEAR_WEIGHT * (
        take_slab(flux_face, 2, extent, which_axis) - take_slab(flux_face, 1, extent, which_axis)
    ) - FAR_WEIGHT * (
        take_slab(flux_face, 3, extent, which_axis) - take_slab(flux_face, 0, extent, which_axis)
    )


def divergence(padded, buoy_pad):
    size_x = padded.shape[-3] - 6
    size_y = padded.shape[-2] - 6
    size_z = padded.shape[-1] - 6
    along_x = axis_term(
        padded[..., 3 : size_y + 3, 3 : size_z + 3],
        buoy_pad[:, 3 : size_y + 3, 3 : size_z + 3],
        size_x,
        -3,
    )
    along_y = axis_term(
        padded[..., 3 : size_x + 3, :, 3 : size_z + 3],
        buoy_pad[3 : size_x + 3, :, 3 : size_z + 3],
        size_y,
        -2,
    )
    along_z = axis_term(
        padded[..., 3 : size_x + 3, 3 : size_y + 3, :],
        buoy_pad[3 : size_x + 3, 3 : size_y + 3, :],
        size_z,
        -1,
    )
    return along_x + along_y + along_z


def sponge_term(coords, length, low_width, high_width):
    position = coords.astype(jnp.float32)
    far_side = length - 1 - position
    low_float = low_width.astype(jnp.float32)
    high_float = high_width.astype(jnp.float32)
    low_part = jnp.where(
        position < low_float, jnp.square(SPONGE_RATE * (low_float - position) / low_float), 0.0
    )
    high_part = jnp.where(
        far_side < high_float, jnp.square(SPONGE_RATE * (high_float - far_side) / high_float), 0.0
    )
    return low_part + high_part


def plane_tables(flat_index, size_x, size_y, size_z, total_y):
    plane_size = total_y * size_z
    global_x = flat_index // plane_size
    global_y = flat_index // size_z % total_y
    global_z = flat_index % size_z
    local_x = global_x - lax.axis_index("px") * size_x
    local_y = global_y - lax.axis_index("py") * size_y
    inside = (local_x >= 0) & (local_x < size_x) & (local_y >= 0) & (local_y < size_y)
    plane_at = jnp.where(inside, local_x * size_y + local_y, -1)
    plane_hot = (plane_at[..., None] == lax.iota(jnp.int32, size_x * size_y)).astype(jnp.float32)
    depth_hot = (global_z[..., None] == lax.iota(jnp.int32, size_z)).astype(jnp.float32)
    return (plane_hot, depth_hot)


def kernel_from(gram_total, particles):
    diag_part = jnp.diagonal(gram_total)
    dist_sq = diag_part[:, None] + diag_part[None, :] - 2.0 * gram_total
    width = jnp.sum(dist_sq) / (particles * (particles - 1)) + EPSILON
    kernel = jnp.exp(-dist_sq / width)
    return (kernel, jnp.sum(kernel, axis=1))


def on_device(
    velocity,
    buoyancy,
    forward_prev,
    forward_now,
    adjoint_prev,
    adjoint_now,
    sources,
    wavelet,
    receivers,
    misfit,
    sponge,
):
    part_dev, size_x, size_y, size_z = velocity.shape
    block_cells = size_x * size_y * size_z
    total_x = size_x * lax.axis_size("px")
    total_y = size_y * lax.axis_size("py")
    total_cells = total_x * total_y * size_z
    particles = part_dev * lax.axis_size("dom")
    step_sq = TIME_STEP * TIME_STEP
    coords_x = lax.iota(jnp.int32, size_x) + lax.axis_index("px") * size_x
    coords_y = lax.iota(jnp.int32, size_y) + lax.axis_index("py") * size_y
    coords_z = lax.iota(jnp.int32, size_z)
    damping = jnp.exp(
        -(
            sponge_term(coords_x, total_x, sponge[0], sponge[1])[:, None, None]
            + sponge_term(coords_y, total_y, sponge[2], sponge[3])[None, :, None]
            + sponge_term(coords_z, size_z, sponge[4], sponge[5])[None, None, :]
        )
    )
    buoy_rim = with_halo(buoyancy, (("px", 0), ("py", 1)), 3)
    buoy_pad = jnp.pad(buoy_rim, ((0, 0), (0, 0), (3, 3)))
    wave_scale = velocity * velocity / buoyancy
    grad_coef = -2.0 / (velocity * velocity * velocity)
    src_plane, src_depth = plane_tables(sources, size_x, size_y, size_z, total_y)
    src_pattern = (src_plane[:, :, None] * src_depth[:, None, :]).reshape(velocity.shape)
    rec_plane, rec_depth = plane_tables(receivers, size_x, size_y, size_z, total_y)
    previous = jnp.stack([forward_prev, adjoint_prev])
    current = jnp.stack([forward_now, adjoint_now])
    gradient = jnp.zeros_like(velocity)
    for step_at in range(wavelet.shape[1]):
        rimmed = with_halo(current, (("px", 2), ("py", 3)), 3)
        padded = jnp.pad(rimmed, ((0, 0), (0, 0), (0, 0), (0, 0), (3, 3)))
        stepped = 2.0 * current - previous + step_sq * (wave_scale * divergence(padded, buoy_pad))
        weighted_depth = rec_depth * (step_sq * misfit[:, step_at, :])[:, :, None]
        rec_field = jnp.einsum(
            "prq,prz->pqz",
            rec_plane,
            weighted_depth,
            precision=lax.Precision.HIGHEST,
            preferred_element_type=jnp.float32,
        )
        src_field = src_pattern * (step_sq * wavelet[:, step_at])[:, None, None, None]
        injected = jnp.stack(
            [stepped[0] + src_field, stepped[1] + rec_field.reshape(velocity.shape)]
        )
        advanced = damping * injected
        gradient = gradient + grad_coef * current[1] * (
            advanced[0] - 2.0 * current[0] + previous[0]
        )
        previous, current = (current, advanced)
    flat_model = velocity.reshape(part_dev, block_cells)
    flat_grad = gradient.reshape(part_dev, block_cells)
    dom_start = lax.axis_index("dom") * part_dev
    own_sq = lax.psum(jnp.sum(flat_grad * flat_grad, axis=1), ("px", "py"))
    flat_grad = flat_grad / jnp.sqrt(own_sq / total_cells + EPSILON)[:, None]
    model_cols, grad_cols = (
        lax.all_to_all(flat_model, "dom", split_axis=1, concat_axis=0, tiled=True),
        lax.all_to_all(flat_grad, "dom", split_axis=1, concat_axis=0, tiled=True),
    )
    centered = model_cols - jnp.mean(model_cols, axis=0, keepdims=True)
    gram_part = jnp.dot(
        centered, centered.T, precision=lax.Precision.HIGHEST, preferred_element_type=jnp.float32
    )
    gram_total = lax.psum(gram_part, ("px", "py", "dom"))
    kernel, row_sum = kernel_from(gram_total, particles)
    mixed_grad = jnp.dot(
        kernel, grad_cols, precision=lax.Precision.HIGHEST, preferred_element_type=jnp.float32
    )
    mixed_model = jnp.dot(
        kernel, model_cols, precision=lax.Precision.HIGHEST, preferred_element_type=jnp.float32
    )
    drift_flat, model_mix = (
        lax.all_to_all(mixed_grad, "dom", split_axis=0, concat_axis=1, tiled=True),
        lax.all_to_all(mixed_model, "dom", split_axis=0, concat_axis=1, tiled=True),
    )
    own_rowsum = lax.dynamic_slice_in_dim(row_sum, dom_start, part_dev)
    spread_flat = flat_model * own_rowsum[:, None] - model_mix
    return (
        previous[0],
        current[0],
        previous[1],
        current[1],
        drift_flat.reshape(velocity.shape),
        spread_flat.reshape(velocity.shape),
    )


def solution(mesh):
    placed = (
        P("dom", "px", "py", None),
        P("px", "py", None),
        P("dom", "px", "py", None),
        P("dom", "px", "py", None),
        P("dom", "px", "py", None),
        P("dom", "px", "py", None),
        P("dom"),
        P("dom", None),
        P("dom", None),
        P("dom", None, None),
        P(),
    )
    return jax.shard_map(
        on_device,
        mesh=mesh,
        in_specs=placed,
        out_specs=(
            P("dom", "px", "py", None),
            P("dom", "px", "py", None),
            P("dom", "px", "py", None),
            P("dom", "px", "py", None),
            P("dom", "px", "py", None),
            P("dom", "px", "py", None),
        ),
        check_vma=False,
    )
```

profile of v0, /device:TPU:1, one launch (start us, length us, event | category | flops | bytes accessed | tf_op | source)
XLA Modules:
  0.0 337.7 jit_solution(8753166672885361764)
XLA Ops:
  0.7 1.8 fusion.117
  2.5 5.1 %collective-permute-start.3 = (f32[2,2,3,32,128]{4,3,2,1,0:T(8,128)}, f32[2,2,3,32,128]{4,3,2,1,0:T(8,128)S(1)}, u32[]{:S(2)}, u32[]{:S(2)}) collective-permute-start(f32[2,2,3,32,128]{4,3,2,1,0:T(8,128)} %get-tuple-element.33), channel_id=1, source_target_pairs={{64,0},{128,64},{192,128},{65,1},{129,65},{193,129},{66,2},{130,66... | collective-permute-start | bytes 589832 | tf_op jit(solution)/shard_map/ppermute | solution.py:23
  7.6 1.9 collective-permute-start.2
  9.5 1.9 collective-permute-start
  11.5 2.4 collective-permute-start.1
  14.1 1.2 copy.54
  15.3 7.7 %all-to-all-start = ((f32[2,8,8192]{2,0,1:T(2,128)}), f32[2,8,8192]{2,0,1:T(2,128)S(1)}, u32[]{:S(2)}, u32[]{:S(2)}) async-start(f32[2,8,8192]{2,0,1:T(2,128)} %copy.54), calls=%async_computation | async-start | bytes 1048576 | tf_op jit(solution)/shard_map/all_to_all | solution.py:184
  28.1 3.2 fusion.2
  31.4 1.3 collective-permute-start.5
  32.7 5.5 %collective-permute-start.4 = (f32[22,3,128]{2,1,0:T(4,128)S(1)}, f32[22,3,128]{2,1,0:T(4,128)S(1)}, u32[]{:S(2)}, u32[]{:S(2)}) collective-permute-start(f32[22,3,128]{2,1,0:T(4,128)S(1)} %get-tuple-element.36), channel_id=1, source_target_pairs={{0,8},{8,16},{16,24},{24,32},{32,40},{40,48},{48,56},{1,9},{9,17},... | collective-permute-start | bytes 101384 | tf_op jit(solution)/shard_map/ppermute | solution.py:21
  41.0 1.3 collective-permute-start.7
  42.3 6.9 %collective-permute-start.6 = (f32[2,2,22,3,128]{4,3,2,1,0:T(4,128)}, f32[2,2,22,3,128]{4,3,2,1,0:T(4,128)}, u32[]{:S(2)}, u32[]{:S(2)}) collective-permute-start(f32[2,2,22,3,128]{4,3,2,1,0:T(4,128)} %get-tuple-element.20), channel_id=1, source_target_pairs={{0,8},{8,16},{16,24},{24,32},{32,40},{40,48},{48,56},{1,9},{9,17},... | collective-permute-start | bytes 405512 | tf_op jit(solution)/shard_map/ppermute | solution.py:21
  49.2 1.2 pad_maximum_fusion.4
  52.1 1.4 sub.399
  54.3 79.6 %psum.14 = f32[16,16]{1,0:T(8,128)S(1)} all-reduce(f32[16,16]{1,0:T(8,128)S(1)} %fusion.141), channel_id=1, replica_groups=mesh['px'=4,'py'=8,'dom'=8] {'px','py','dom'}, use_global_device_ids=true, to_apply=%region_1.2 | all-reduce | flops 256 | bytes 2048 | tf_op jit(solution)/shard_map/psum | solution.py:191
  137.9 5.5 %all-to-all-start.3 = ((f32[8,2,8192]{2,1,0:T(2,128)}), f32[8,2,8192]{2,1,0:T(2,128)}, u32[]{:S(2)}, u32[]{:S(2)}) async-start(f32[8,2,8192]{2,1,0:T(2,128)} %copy.60), calls=%async_computation.3 | async-start | bytes 1048576 | tf_op jit(solution)/shard_map/all_to_all | solution.py:201
  143.3 2.4 fusion.47
  145.8 1.3 pad_maximum_fusion
  147.1 3.1 fusion.6
  150.2 2.6 fusion.37
  152.8 8.6 %all-to-all-done.3 = f32[8,2,8192]{2,1,0:T(2,128)} async-done(((f32[8,2,8192]{2,1,0:T(2,128)}), f32[8,2,8192]{2,1,0:T(2,128)}, u32[]{:S(2)}, u32[]{:S(2)}) %all-to-all-start.3) | async-done | bytes 524320 | tf_op jit(solution)/shard_map/all_to_all | solution.py:201
  161.4 2.1 copy.61
  163.5 1.9 all_to_all.59
  165.5 2.4 multiply_subtract_fusion
  167.8 4.3 %fusion.84 = f32[2,2,16,32,128]{4,3,2,1,0:T(8,128)S(1)} fusion(f32[2,2,16,32,131]{4,3,2,1,0:T(8,128)} %fusion.6, f32[2,2,16,35,128]{4,3,2,1,0:T(8,128)S(1)} %copy-done.2, f32[2,2,19,32,128]{4,3,2,1,0:T(8,128)S(1)} %fusion.47, f32[1,2,16,32,128]{4,3,2,1,0:T(8,128)S(1)} %bitcast.82, f32[1,2,16,32,128]{4,3,2,1,0:T(8,128)S(1)} %bitcast.81, ...), kind=kLoop, calls=%fused_computation.153 | loop fusion | flops 6291456 | bytes 16252928 | tf_op jit(solution)/shard_map/add | solution.py:160
  172.6 2.4 collective-permute-start.9
  175.0 3.2 collective-permute-start.8
  178.2 2.5 fusion.1
  180.8 1.3 collective-permute-start.11
  182.1 5.6 %collective-permute-start.10 = (f32[2,2,22,3,128]{4,3,2,1,0:T(4,128)S(1)}, f32[2,2,22,3,128]{4,3,2,1,0:T(4,128)S(1)}, u32[]{:S(2)}, u32[]{:S(2)}) collective-permute-start(f32[2,2,22,3,128]{4,3,2,1,0:T(4,128)S(1)} %get-tuple-element.18), channel_id=1, source_target_pairs={{0,8},{8,16},{16,24},{24,32},{32,40},{40,48},{48,56},{1,9},{9,17},... | collective-permute-start | bytes 405512 | tf_op jit(solution)/shard_map/ppermute | solution.py:21
  188.3 1.9 collective-permute-done.11
  190.2 2.4 collective-permute-done.10
  192.9 1.7 fusion.12
  195.2 1.3 fusion.70
  196.9 2.3 collective-permute-start.13
  199.2 3.5 %collective-permute-start.12 = (f32[2,2,3,32,128]{4,3,2,1,0:T(8,128)S(1)}, f32[2,2,3,32,128]{4,3,2,1,0:T(8,128)S(1)}, u32[]{:S(2)}, u32[]{:S(2)}) collective-permute-start(f32[2,2,3,32,128]{4,3,2,1,0:T(8,128)S(1)} %get-tuple-element.24), channel_id=1, source_target_pairs={{0,64},{64,128},{128,192},{1,65},{65,129},{129,193},{2,66},{66,130... | collective-permute-start | bytes 589832 | tf_op jit(solution)/shard_map/ppermute | solution.py:21
  202.7 2.5 fusion
  205.3 1.3 collective-permute-start.15
  206.6 6.3 %collective-permute-start.14 = (f32[2,2,22,3,128]{4,3,2,1,0:T(4,128)S(1)}, f32[2,2,22,3,128]{4,3,2,1,0:T(4,128)S(1)}, u32[]{:S(2)}, u32[]{:S(2)}) collective-permute-start(f32[2,2,22,3,128]{4,3,2,1,0:T(4,128)S(1)} %get-tuple-element.16), channel_id=1, source_target_pairs={{0,8},{8,16},{16,24},{24,32},{32,40},{40,48},{48,56},{1,9},{9,17},... | collective-permute-start | bytes 405512 | tf_op jit(solution)/shard_map/ppermute | solution.py:21
  213.4 1.6 collective-permute-done.15
  215.1 4.6 %collective-permute-done.14 = f32[2,2,22,3,128]{4,3,2,1,0:T(4,128)S(1)} collective-permute-done((f32[2,2,22,3,128]{4,3,2,1,0:T(4,128)S(1)}, f32[2,2,22,3,128]{4,3,2,1,0:T(4,128)S(1)}, u32[]{:S(2)}, u32[]{:S(2)}) %collective-permute-start.14) | collective-permute-done | bytes 135200 | tf_op jit(solution)/shard_map/ppermute | solution.py:21
  220.0 1.7 fusion.18
  222.3 1.3 fusion.56
  224.8 1.6 multiply_reduce_fusion
  226.5 68.9 %psum.15 = f32[2]{0:T(128)S(1)} all-reduce(f32[2]{0:T(128)S(1)} %get-tuple-element.11), channel_id=1, replica_groups=mesh['px'=4,'py'=8,'dom'=8] {'px','py'}, use_global_device_ids=true, to_apply=%region_4.5 | all-reduce | flops 2 | bytes 16 | tf_op jit(solution)/shard_map/psum | solution.py:181
  295.9 19.1 %all_to_all.64 = f32[2,8,8192]{2,0,1:T(2,128)S(1)} all-to-all(f32[2,8,8192]{2,0,1:T(2,128)S(1)} %copy.55), channel_id=1, replica_groups=mesh['px'=4,'py'=8,'dom'=8] {'dom'}, dimensions={1} | all-to-all | bytes 1048576 | tf_op jit(solution)/shard_map/all_to_all | solution.py:185
  317.1 3.5 %all-to-all-start.2 = ((f32[8,2,8192]{2,1,0:T(2,128)}), f32[8,2,8192]{2,1,0:T(2,128)S(1)}, u32[]{:S(2)}, u32[]{:S(2)}) async-start(f32[8,2,8192]{2,1,0:T(2,128)} %copy.57), calls=%async_computation.2 | async-start | bytes 1048576 | tf_op jit(solution)/shard_map/all_to_all | solution.py:200
  321.5 15.1 %all-to-all-done.2 = f32[8,2,8192]{2,1,0:T(2,128)S(1)} async-done(((f32[8,2,8192]{2,1,0:T(2,128)}), f32[8,2,8192]{2,1,0:T(2,128)S(1)}, u32[]{:S(2)}, u32[]{:S(2)}) %all-to-all-start.2) | async-done | bytes 524320 | tf_op jit(solution)/shard_map/all_to_all | solution.py:200
  (115 shorter events, 19.9 us)
Async XLA Ops:
  0.6 8.9 %copy-start.11 = (f32[16,32,128]{2,1,0:T(8,128)S(1)}, f32[16,32,128]{2,1,0:T(8,128)}, u32[]{:S(2)}) copy-start(f32[16,32,128]{2,1,0:T(8,128)} %param.12) | copy-start | bytes 786436
  0.6 13.2 %copy-start.8 = (f32[2,16,32,128]{3,2,1,0:T(8,128)S(1)}, f32[2,16,32,128]{3,2,1,0:T(8,128)}, u32[]{:S(2)}) copy-start(f32[2,16,32,128]{3,2,1,0:T(8,128)} %param.11) | copy-start | bytes 1572868
  2.5 37.4 %collective-permute-start.3 = (f32[2,2,3,32,128]{4,3,2,1,0:T(8,128)}, f32[2,2,3,32,128]{4,3,2,1,0:T(8,128)S(1)}, u32[]{:S(2)}, u32[]{:S(2)}) collective-permute-start(f32[2,2,3,32,128]{4,3,2,1,0:T(8,128)} %get-tuple-element.33), channel_id=1, source_target_pairs={{64,0},{128,64},{192,128},{65,1},{129,65},{193,129},{66,2},{130,66... | collective-permute-start | bytes 589832 | tf_op jit(solution)/shard_map/ppermute | solution.py:23
  7.6 32.3 %collective-permute-start.2 = (f32[2,2,3,32,128]{4,3,2,1,0:T(8,128)S(1)}, f32[2,2,3,32,128]{4,3,2,1,0:T(8,128)S(1)}, u32[]{:S(2)}, u32[]{:S(2)}) collective-permute-start(f32[2,2,3,32,128]{4,3,2,1,0:T(8,128)S(1)} %get-tuple-element.32), channel_id=1, source_target_pairs={{0,64},{64,128},{128,192},{1,65},{65,129},{129,193},{2,66},{66,130... | collective-permute-start | bytes 589832 | tf_op jit(solution)/shard_map/ppermute | solution.py:21
  9.5 21.8 %collective-permute-start = (f32[3,32,128]{2,1,0:T(8,128)S(1)}, f32[3,32,128]{2,1,0:T(8,128)S(1)}, u32[]{:S(2)}, u32[]{:S(2)}) collective-permute-start(f32[3,32,128]{2,1,0:T(8,128)S(1)} %get-tuple-element.39), channel_id=1, source_target_pairs={{0,64},{64,128},{128,192},{1,65},{65,129},{129,193},{2,66},{66,130... | collective-permute-start | bytes 147464 | tf_op jit(solution)/shard_map/ppermute | solution.py:21
  11.5 19.9 %collective-permute-start.1 = (f32[3,32,128]{2,1,0:T(8,128)S(1)}, f32[3,32,128]{2,1,0:T(8,128)S(1)}, u32[]{:S(2)}, u32[]{:S(2)}) collective-permute-start(f32[3,32,128]{2,1,0:T(8,128)S(1)} %get-tuple-element.38), channel_id=1, source_target_pairs={{64,0},{128,64},{192,128},{65,1},{129,65},{193,129},{66,2},{130,66... | collective-permute-start | bytes 147464 | tf_op jit(solution)/shard_map/ppermute | solution.py:23
  14.0 8.9 %copy-start.16 = (f32[2,3]{1,0:T(2,128)S(1)}, f32[2,3]{1,0:T(2,128)}, u32[]{:S(2)}) copy-start(f32[2,3]{1,0:T(2,128)} %param.18) | copy-start | bytes 76
  14.0 9.2 %copy-start.18 = (s32[2]{0:T(128)S(1)}, s32[2]{0:T(128)}, u32[]{:S(2)}) copy-start(s32[2]{0:T(128)} %param.17) | copy-start | bytes 28
  14.0 9.3 %copy-start.17 = (s32[2,1024]{1,0:T(2,128)S(1)}, s32[2,1024]{1,0:T(2,128)}, u32[]{:S(2)}) copy-start(s32[2,1024]{1,0:T(2,128)} %param.19) | copy-start | bytes 24580
  14.0 9.3 %copy-start.14 = (f32[2,3,1024]{2,0,1:T(2,128)S(1)}, f32[2,3,1024]{2,0,1:T(2,128)}, u32[]{:S(2)}) copy-start(f32[2,3,1024]{2,0,1:T(2,128)} %param.20) | copy-start | bytes 73732
  14.0 9.3 %copy-start.15 = (s32[6]{0:T(128)S(1)}, s32[6]{0:T(128)}, u32[]{:S(2)}) copy-start(s32[6]{0:T(128)} %param.21) | copy-start | bytes 76
  15.3 35.2 %all-to-all-start = ((f32[2,8,8192]{2,0,1:T(2,128)}), f32[2,8,8192]{2,0,1:T(2,128)S(1)}, u32[]{:S(2)}, u32[]{:S(2)}) async-start(f32[2,8,8192]{2,0,1:T(2,128)} %copy.54), calls=%async_computation | async-start | bytes 1048576 | tf_op jit(solution)/shard_map/all_to_all | solution.py:184
  31.4 7.6 %collective-permute-start.5 = (f32[22,3,128]{2,1,0:T(4,128)S(1)}, f32[22,3,128]{2,1,0:T(4,128)S(1)}, u32[]{:S(2)}, u32[]{:S(2)}) collective-permute-start(f32[22,3,128]{2,1,0:T(4,128)S(1)} %get-tuple-element.37), channel_id=1, source_target_pairs={{8,0},{16,8},{24,16},{32,24},{40,32},{48,40},{56,48},{9,1},{17,9},... | collective-permute-start | bytes 101384 | tf_op jit(solution)/shard_map/ppermute | solution.py:23
  32.7 6.6 %collective-permute-start.4 = (f32[22,3,128]{2,1,0:T(4,128)S(1)}, f32[22,3,128]{2,1,0:T(4,128)S(1)}, u32[]{:S(2)}, u32[]{:S(2)}) collective-permute-start(f32[22,3,128]{2,1,0:T(4,128)S(1)} %get-tuple-element.36), channel_id=1, source_target_pairs={{0,8},{8,16},{16,24},{24,32},{32,40},{40,48},{48,56},{1,9},{9,17},... | collective-permute-start | bytes 101384 | tf_op jit(solution)/shard_map/ppermute | solution.py:21
  39.0 1.0 copy-start
  39.0 1.2 copy-start.1
  39.9 10.6 %copy-start.4 = (f32[2,2,3,32,128]{4,3,2,1,0:T(8,128)}, f32[2,2,3,32,128]{4,3,2,1,0:T(8,128)S(1)}, u32[]{:S(2)}) copy-start(f32[2,2,3,32,128]{4,3,2,1,0:T(8,128)S(1)} %collective-permute-done.3) | copy-start | bytes 589828
  40.2 10.3 %copy-start.6 = (f32[2,2,3,32,128]{4,3,2,1,0:T(8,128)}, f32[2,2,3,32,128]{4,3,2,1,0:T(8,128)S(1)}, u32[]{:S(2)}) copy-start(f32[2,2,3,32,128]{4,3,2,1,0:T(8,128)S(1)} %collective-permute-done.2) | copy-start | bytes 589828
  41.0 104.7 %collective-permute-start.7 = (f32[2,2,22,3,128]{4,3,2,1,0:T(4,128)}, f32[2,2,22,3,128]{4,3,2,1,0:T(4,128)}, u32[]{:S(2)}, u32[]{:S(2)}) collective-permute-start(f32[2,2,22,3,128]{4,3,2,1,0:T(4,128)} %get-tuple-element.21), channel_id=1, source_target_pairs={{8,0},{16,8},{24,16},{32,24},{40,32},{48,40},{56,48},{9,1},{17,9},... | collective-permute-start | bytes 405512 | tf_op jit(solution)/shard_map/ppermute | solution.py:23
  42.3 103.5 %collective-permute-start.6 = (f32[2,2,22,3,128]{4,3,2,1,0:T(4,128)}, f32[2,2,22,3,128]{4,3,2,1,0:T(4,128)}, u32[]{:S(2)}, u32[]{:S(2)}) collective-permute-start(f32[2,2,22,3,128]{4,3,2,1,0:T(4,128)} %get-tuple-element.20), channel_id=1, source_target_pairs={{0,8},{8,16},{16,24},{24,32},{32,40},{40,48},{48,56},{1,9},{9,17},... | collective-permute-start | bytes 405512 | tf_op jit(solution)/shard_map/ppermute | solution.py:21
  137.9 23.5 %all-to-all-start.3 = ((f32[8,2,8192]{2,1,0:T(2,128)}), f32[8,2,8192]{2,1,0:T(2,128)}, u32[]{:S(2)}, u32[]{:S(2)}) async-start(f32[8,2,8192]{2,1,0:T(2,128)} %copy.60), calls=%async_computation.3 | async-start | bytes 1048576 | tf_op jit(solution)/shard_map/all_to_all | solution.py:201
  143.3 2.5 copy-start.5
  143.3 2.5 copy-start.7
  165.4 2.4 copy-start.2
  165.4 2.4 copy-start.10
  165.5 2.4 copy-start.12
  167.8 4.3 %copy-start.13 = (f32[2,512,128]{2,1,0:T(8,128)S(1)}, f32[2,512,128]{2,1,0:T(8,128)}, u32[]{:S(2)}) copy-start(f32[2,512,128]{2,1,0:T(8,128)} %fusion.2) | copy-start | bytes 1572868
  172.6 8.1 %collective-permute-start.9 = (f32[2,2,3,32,128]{4,3,2,1,0:T(8,128)S(1)}, f32[2,2,3,32,128]{4,3,2,1,0:T(8,128)S(1)}, u32[]{:S(2)}, u32[]{:S(2)}) collective-permute-start(f32[2,2,3,32,128]{4,3,2,1,0:T(8,128)S(1)} %get-tuple-element.29), channel_id=1, source_target_pairs={{64,0},{128,64},{192,128},{65,1},{129,65},{193,129},{66,2},{130,66... | collective-permute-start | bytes 589832 | tf_op jit(solution)/shard_map/ppermute | solution.py:23
  175.0 5.8 %collective-permute-start.8 = (f32[2,2,3,32,128]{4,3,2,1,0:T(8,128)S(1)}, f32[2,2,3,32,128]{4,3,2,1,0:T(8,128)S(1)}, u32[]{:S(2)}, u32[]{:S(2)}) collective-permute-start(f32[2,2,3,32,128]{4,3,2,1,0:T(8,128)S(1)} %get-tuple-element.28), channel_id=1, source_target_pairs={{0,64},{64,128},{128,192},{1,65},{65,129},{129,193},{2,66},{66,130... | collective-permute-start | bytes 589832 | tf_op jit(solution)/shard_map/ppermute | solution.py:21
  180.8 9.3 %collective-permute-start.11 = (f32[2,2,22,3,128]{4,3,2,1,0:T(4,128)S(1)}, f32[2,2,22,3,128]{4,3,2,1,0:T(4,128)S(1)}, u32[]{:S(2)}, u32[]{:S(2)}) collective-permute-start(f32[2,2,22,3,128]{4,3,2,1,0:T(4,128)S(1)} %get-tuple-element.19), channel_id=1, source_target_pairs={{8,0},{16,8},{24,16},{32,24},{40,32},{48,40},{56,48},{9,1},{17,9},... | collective-permute-start | bytes 405512 | tf_op jit(solution)/shard_map/ppermute | solution.py:23
  182.1 5.8 %copy-start.3 = (f32[19,32,128]{2,1,0:T(8,128)S(1)}, f32[19,32,128]{2,1,0:T(8,128)}, u32[]{:S(2)}) copy-start(f32[19,32,128]{2,1,0:T(8,128)} %fusion.116) | copy-start | bytes 933892
  182.1 10.5 %collective-permute-start.10 = (f32[2,2,22,3,128]{4,3,2,1,0:T(4,128)S(1)}, f32[2,2,22,3,128]{4,3,2,1,0:T(4,128)S(1)}, u32[]{:S(2)}, u32[]{:S(2)}) collective-permute-start(f32[2,2,22,3,128]{4,3,2,1,0:T(4,128)S(1)} %get-tuple-element.18), channel_id=1, source_target_pairs={{0,8},{8,16},{16,24},{24,32},{32,40},{40,48},{48,56},{1,9},{9,17},... | collective-permute-start | bytes 405512 | tf_op jit(solution)/shard_map/ppermute | solution.py:21
  196.9 8.3 %collective-permute-start.13 = (f32[2,2,3,32,128]{4,3,2,1,0:T(8,128)S(1)}, f32[2,2,3,32,128]{4,3,2,1,0:T(8,128)S(1)}, u32[]{:S(2)}, u32[]{:S(2)}) collective-permute-start(f32[2,2,3,32,128]{4,3,2,1,0:T(8,128)S(1)} %get-tuple-element.25), channel_id=1, source_target_pairs={{64,0},{128,64},{192,128},{65,1},{129,65},{193,129},{66,2},{130,66... | collective-permute-start | bytes 589832 | tf_op jit(solution)/shard_map/ppermute | solution.py:23
  199.2 6.0 %collective-permute-start.12 = (f32[2,2,3,32,128]{4,3,2,1,0:T(8,128)S(1)}, f32[2,2,3,32,128]{4,3,2,1,0:T(8,128)S(1)}, u32[]{:S(2)}, u32[]{:S(2)}) collective-permute-start(f32[2,2,3,32,128]{4,3,2,1,0:T(8,128)S(1)} %get-tuple-element.24), channel_id=1, source_target_pairs={{0,64},{64,128},{128,192},{1,65},{65,129},{129,193},{2,66},{66,130... | collective-permute-start | bytes 589832 | tf_op jit(solution)/shard_map/ppermute | solution.py:21
  205.3 9.8 %collective-permute-start.15 = (f32[2,2,22,3,128]{4,3,2,1,0:T(4,128)S(1)}, f32[2,2,22,3,128]{4,3,2,1,0:T(4,128)S(1)}, u32[]{:S(2)}, u32[]{:S(2)}) collective-permute-start(f32[2,2,22,3,128]{4,3,2,1,0:T(4,128)S(1)} %get-tuple-element.17), channel_id=1, source_target_pairs={{8,0},{16,8},{24,16},{32,24},{40,32},{48,40},{56,48},{9,1},{17,9},... | collective-permute-start | bytes 405512 | tf_op jit(solution)/shard_map/ppermute | solution.py:23
  206.6 13.1 %collective-permute-start.14 = (f32[2,2,22,3,128]{4,3,2,1,0:T(4,128)S(1)}, f32[2,2,22,3,128]{4,3,2,1,0:T(4,128)S(1)}, u32[]{:S(2)}, u32[]{:S(2)}) collective-permute-start(f32[2,2,22,3,128]{4,3,2,1,0:T(4,128)S(1)} %get-tuple-element.16), channel_id=1, source_target_pairs={{0,8},{8,16},{16,24},{24,32},{32,40},{40,48},{48,56},{1,9},{9,17},... | collective-permute-start | bytes 405512 | tf_op jit(solution)/shard_map/ppermute | solution.py:21
  223.8 1.0 copy-start.9
  317.1 19.4 %all-to-all-start.2 = ((f32[8,2,8192]{2,1,0:T(2,128)}), f32[8,2,8192]{2,1,0:T(2,128)S(1)}, u32[]{:S(2)}, u32[]{:S(2)}) async-start(f32[8,2,8192]{2,1,0:T(2,128)} %copy.57), calls=%async_computation.2 | async-start | bytes 1048576 | tf_op jit(solution)/shard_map/all_to_all | solution.py:200
where the time goes:
time: 339 us; the launch traced here: 338 us
  blocking collectives  168 us (50%)
  starting transfers between devices  68.8 us (20%)
  other arithmetic  35.5 us (10%)
  waiting for transfers between devices  34.7 us (10%)
  local copies, waits for them, and re-layouts  15.2 us (4%)
  matrix products  10.2 us (3%)
  between operations  5.78 us (2%)
    psum x1, blocking collectives, on_device(): gram_total = lax.psum(gram_part, ('px', 'py', 'dom'))  79.6 us
    psum x1, blocking collectives, on_device(): own_sq = lax.psum(jnp.sum(flat_grad * flat_grad, axis=1), ('px', 'py'))  68.9 us
    ppermute x8, starting transfers between devices, with_halo(): lax.ppermute(tail, axis, [(i, (i + 1) % count) for i in range(ends)])  34.8 us
    all_to_all x1, blocking collectives, on_device(): lax.all_to_all(flat_grad, 'dom', split_axis=1, concat_axis=0, tiled=True)  19.1 us
    ppermute x8, starting transfers between devices, with_halo(): lax.ppermute(head, axis, [((i + 1) % count, i) for i in range(ends)])  17.4 us
    all_to_all x1, waiting for transfers between devices, on_device(): lax.all_to_all(mixed_grad, 'dom', split_axis=0, concat_axis=1, tiled=True)  15.1 us
    mul x9, other arithmetic, axis_term(): flux_face = half_buoy * slope_face  13.4 us
    all_to_all x1, waiting for transfers between devices, on_device(): lax.all_to_all(mixed_model, 'dom', split_axis=0, concat_axis=1, tiled=True)  8.58 us
  transfers between devices with their start and end apart: 19, of which 8 were waited for; matrix products, arithmetic and copies ran while one was open for 10% of the time, Pallas kernels for 0%

commit v1 on v0

v1 whole, which is shorter than its diff:
```python
import functools

import jax
import jax.numpy as jnp
from jax import lax
from jax.experimental import pallas as pl
from jax.experimental.pallas import tpu as pltpu
from jax.sharding import PartitionSpec as P

EPSILON = 1e-06
TIME_STEP = 0.18
STEP_SQ = TIME_STEP * TIME_STEP
SPONGE_RATE = 0.5
NEAR = 9.0 / 8.0
FAR = 1.0 / 24.0
MESH = pl.DeviceIdType.MESH
F32 = jnp.float32
BF16 = jnp.bfloat16
HIGHEST = lax.Precision.HIGHEST
NT = (((1,), (1,)), ((), ()))
EDGE = 3
TOP = 8


def sponge_part(position, length, low, high):
    far_side = (length - 1) - position
    low_part = jnp.where(position < low, jnp.square(SPONGE_RATE * (low - position) / low), 0.0)
    high_part = jnp.where(far_side < high, jnp.square(SPONGE_RATE * (high - far_side) / high), 0.0)
    return low_part + high_part


def axis_coefs(faces):
    below2, below, here, above = faces
    near_sq, cross, far_sq = NEAR * NEAR, NEAR * FAR, FAR * FAR
    return (
        -near_sq * (here + below) - far_sq * (above + below2),
        near_sq * here + cross * (below + above),
        near_sq * below + cross * (here + below2),
        -cross * (here + above),
        -cross * (below + below2),
        far_sq * above,
        far_sq * below2,
    )


SHIFTS = (1, -1, 2, -2, 3, -3)


def kernel(
    counts,
    vel_in,
    buoy_in,
    fp_in,
    fn_in,
    ap_in,
    an_in,
    sources,
    wavelet,
    receivers,
    misfit,
    sponge,
    fb_out,
    fa_out,
    ab_out,
    aa_out,
    drift_out,
    spread_out,
    S,
    vel,
    bpad,
    C,
    damp,
    src_hot,
    inj,
    b_hi,
    b_lo,
    grad,
    mcols,
    gcols,
    mix_m,
    mix_g,
    T,
    KB,
    gram_px,
    gram_py,
    gram_dom,
    norm_px,
    norm_py,
    norm_dom,
    load_sem,
    halo_send,
    halo_recv,
    col_send,
    col_recv,
    sum_send,
    sum_recv,
    out_sem,
):
    n_px, n_py, n_dom = counts
    parts, size_x, size_y, size_z = vel.shape
    steps = wavelet.shape[1]
    tiles = size_y // 8
    px, py, dom = lax.axis_index("px"), lax.axis_index("py"), lax.axis_index("dom")
    coord = {"px": px, "py": py, "dom": dom}
    count = {"px": n_px, "py": n_py, "dom": n_dom}
    total_x, total_y = size_x * n_px, size_y * n_py
    particles = parts * n_dom
    share = size_x // n_dom
    cells = pl.ds(EDGE, size_x), pl.ds(TOP, size_y)
    row8 = lax.broadcasted_iota(jnp.int32, (8, size_z), 0)
    lane8 = lax.broadcasted_iota(jnp.int32, (8, size_z), 1)

    def peer(axis, k):
        return lax.rem(coord[axis] + k, count[axis])

    barrier = pltpu.get_barrier_semaphore()
    for axis in ("px", "py", "dom"):
        for k in range(1, count[axis]):
            pl.semaphore_signal(barrier, inc=1, device_id={axis: peer(axis, k)}, device_id_type=MESH)

    loads = [
        pltpu.make_async_copy(vel_in, vel, load_sem.at[0]),
        pltpu.make_async_copy(buoy_in, bpad.at[cells], load_sem.at[1]),
        pltpu.make_async_copy(fn_in, S.at[(1, pl.ds(0, parts)) + cells], load_sem.at[2]),
        pltpu.make_async_copy(an_in, S.at[(1, pl.ds(parts, parts)) + cells], load_sem.at[3]),
        pltpu.make_async_copy(fp_in, S.at[(0, pl.ds(0, parts)) + cells], load_sem.at[4]),
        pltpu.make_async_copy(ap_in, S.at[(0, pl.ds(parts, parts)) + cells], load_sem.at[5]),
    ]
    for copy in loads:
        copy.start()

    zero_rows = jnp.zeros((8, size_z), F32)
    zero_plane = jnp.zeros((size_y, size_z), F32)

    def zero_planes(first):
        for k in range(EDGE):
            bpad[first + k, pl.ds(TOP, size_y), :] = zero_plane
            for state in range(1, 1 + steps):
                for f in range(2 * parts):
                    S[state, f, first + k, pl.ds(TOP, size_y), :] = zero_plane

    def zero_strip(first):
        def body(x, carry):
            bpad[x, pl.ds(first, 8), :] = zero_rows
            for state in range(1, 1 + steps):
                for f in range(2 * parts):
                    S[state, f, x, pl.ds(first, 8), :] = zero_rows
            return carry

        lax.fori_loop(EDGE, EDGE + size_x, body, 0)

    pl.when(px == 0)(lambda: zero_planes(0))
    pl.when(px == n_px - 1)(lambda: zero_planes(EDGE + size_x))
    pl.when(py == 0)(lambda: zero_strip(0))
    pl.when(py == n_py - 1)(lambda: zero_strip(TOP + size_y))

    def halo_copies(ref, lead, group):
        def at(x, y):
            return ref.at[lead + (x, y)]

        x_all, y_all = cells
        last_x, last_y = EDGE + size_x, TOP + size_y
        moves = (
            ("px", 1, at(pl.ds(last_x - EDGE, EDGE), y_all), at(pl.ds(0, EDGE), y_all)),
            ("px", -1, at(pl.ds(EDGE, EDGE), y_all), at(pl.ds(last_x, EDGE), y_all)),
            ("py", 1, at(x_all, pl.ds(last_y - EDGE, EDGE)), at(x_all, pl.ds(TOP - EDGE, EDGE))),
            ("py", -1, at(x_all, pl.ds(TOP, EDGE)), at(x_all, pl.ds(last_y, EDGE))),
        )
        copies = []
        for way, (axis, k, src, dst) in enumerate(moves):
            copies.append(
                pltpu.make_async_remote_copy(
                    src,
                    dst,
                    halo_send.at[group, way],
                    halo_recv.at[group, way],
                    device_id={axis: peer(axis, k + count[axis])},
                    device_id_type=MESH,
                )
            )
        can_send = (px < n_px - 1, px > 0, py < n_py - 1, py > 0)
        can_recv = (px > 0, px < n_px - 1, py > 0, py < n_py - 1)
        return copies, can_send, can_recv

    def send_halo(halo):
        copies, can_send, _ = halo
        for way in (2, 3, 0, 1):
            pl.when(can_send[way])(copies[way].start)

    def wait_halo(halo):
        copies, can_send, can_recv = halo
        for way in range(4):
            pl.when(can_send[way])(copies[way].wait_send)
            pl.when(can_recv[way])(copies[way].wait_recv)

    halo_b = halo_copies(bpad, (), 0)
    halo_w = {
        (state, kind): halo_copies(S, (state, pl.ds(kind * parts, parts)), 2 * state - 1 + kind)
        for state in range(1, 1 + steps)
        for kind in range(2)
    }

    def column_copies(values, cols, lane):
        return [
            pltpu.make_async_remote_copy(
                values.at[:, pl.ds(peer("dom", k) * share, share)],
                cols.at[pl.ds(dom * parts, parts)],
                col_send.at[lane, k],
                col_recv.at[lane, k],
                device_id={"dom": peer("dom", k)},
                device_id_type=MESH,
            )
            for k in range(1, n_dom)
        ]

    def own_column(values, cols, lane):
        return pltpu.make_async_copy(
            values.at[:, pl.ds(dom * share, share)], cols.at[pl.ds(dom * parts, parts)], col_send.at[lane, 0]
        )

    slots = []
    for _ in range(2):
        for axis in ("px", "py", "dom"):
            slots.append(axis)

    def sum_copies(buffer, axis, slot):
        return [
            pltpu.make_async_remote_copy(
                buffer.at[coord[axis]],
                buffer.at[coord[axis]],
                sum_send.at[slot, k],
                sum_recv.at[slot, k],
                device_id={axis: peer(axis, k)},
                device_id_type=MESH,
            )
            for k in range(1, count[axis])
        ]

    def sum_send_off(buffer, axis, slot, value):
        buffer[coord[axis]] = value
        for copy in sum_copies(buffer, axis, slot):
            copy.start()

    def sum_gather(buffer, axis, slot):
        for copy in sum_copies(buffer, axis, slot):
            copy.wait()
        value = buffer[0]
        for k in range(1, count[axis]):
            value = value + buffer[k]
        return value

    def wave_step(step, kind):
        now, before, later = step + 1, step, step + 2
        last = step == steps - 1

        def plane(x, carry):
            sums = list(carry)
            for t in range(tiles):
                rows = pl.ds(8 * t, 8)
                weights = [C[k, x, rows, :] for k in range(19)]
                fade = damp[x, rows, :]
                for p in range(parts):
                    f = kind * parts + p
                    here = S[now, f, x + EDGE, pl.ds(TOP + 8 * t, 8), :]
                    along_x = [S[now, f, x + EDGE + k, pl.ds(TOP + 8 * t, 8), :] for k in SHIFTS]
                    along_y = [S[now, f, x + EDGE, pl.ds(TOP + 8 * t + k, 8), :] for k in SHIFTS]
                    along_z = [pltpu.roll(here, (size_z - k) % size_z, 1) for k in SHIFTS]
                    terms = [weights[0] * here]
                    for base, values in ((1, along_x), (7, along_y), (13, along_z)):
                        part = None
                        for k, value in enumerate(values):
                            term = weights[base + k] * value
                            part = term if part is None else part + term
                        terms.append(part)
                    lap = (terms[0] + terms[1]) + (terms[2] + terms[3])
                    speed = vel[p, x, rows, :]
                    old = S[before, f, x + EDGE, pl.ds(TOP + 8 * t, 8), :]
                    bend = old - 2.0 * here
                    new = (speed * speed) * lap - bend
                    if kind == 0:
                        new = new + src_hot[p, x, rows, :] * (STEP_SQ * wavelet[p, step])
                    else:
                        new = new + inj[step, p, pl.ds(pl.multiple_of(x * size_y, size_y) + 8 * t, 8), :]
                    new = fade * new
                    S[later, f, x + EDGE, pl.ds(TOP + 8 * t, 8), :] = new
                    if kind == 0:
                        other = S[now, parts + p, x + EDGE, pl.ds(TOP + 8 * t, 8), :]
                        add = other * (new + bend)
                        if step > 0:
                            add = add + grad[p, x, rows, :]
                        if last:
                            add = add * (-2.0 / (speed * speed * speed))
                            sums[p] = sums[p] + add * add
                        grad[p, x, rows, :] = add
            return tuple(sums)

        start = tuple(jnp.zeros((8, size_z), F32) for _ in range(parts)) if kind == 0 and last else ()
        return lax.fori_loop(0, size_x, plane, start)

    for copy in loads[:4]:
        copy.wait()
    pl.semaphore_wait(barrier, (n_px - 1) + (n_py - 1) + (n_dom - 1))
    send_halo(halo_b)
    send_halo(halo_w[1, 0])
    send_halo(halo_w[1, 1])
    model_moves = column_copies(vel, mcols, 0)
    for copy in model_moves:
        copy.start()
    model_own = own_column(vel, mcols, 0)
    model_own.start()

    widths = [sponge[k].astype(F32) for k in range(6)]
    base_x, base_y = px * size_x, py * size_y
    fade_yz = [
        sponge_part((row8 + (8 * t + base_y)).astype(F32), float(total_y), widths[2], widths[3])
        + sponge_part(lane8.astype(F32), float(size_z), widths[4], widths[5])
        for t in range(tiles)
    ]

    def tables(x, carry):
        at_x = jnp.full((8, size_z), x + base_x, jnp.int32)
        fade_x = sponge_part(at_x.astype(F32), float(total_x), widths[0], widths[1])
        for t in range(tiles):
            rows = pl.ds(8 * t, 8)
            damp[x, rows, :] = jnp.exp(-(fade_x + fade_yz[t]))
            flat = (at_x * total_y + (row8 + (8 * t + base_y))) * size_z + lane8
            for p in range(parts):
                src_hot[p, x, rows, :] = jnp.where(flat == sources[p], 1.0, 0.0)
        return carry

    lax.fori_loop(0, size_x, tables, 0)

    z_bits, y_bits = size_z.bit_length() - 1, total_y.bit_length() - 1
    n_recv = receivers.shape[1]
    for p in range(parts):
        index = receivers[pl.ds(p, 1), :]
        local_x = (index >> (z_bits + y_bits)) - base_x
        local_y = ((index >> z_bits) & (total_y - 1)) - base_y
        depth = index & (size_z - 1)
        inside = (local_x >= 0) & (local_x < size_x) & (local_y >= 0) & (local_y < size_y)
        at_plane = jnp.where(inside, local_x * size_y + local_y, -1)
        hit = lax.broadcasted_iota(jnp.int32, (size_z, n_recv), 0) == depth
        for s in range(steps):
            amount = STEP_SQ * misfit[p, pl.ds(s, 1), :]
            high = amount.astype(BF16).astype(F32)
            b_hi[s] = jnp.where(hit, high, 0.0).astype(BF16)
            b_lo[s] = jnp.where(hit, amount - high, 0.0).astype(BF16)

        def spread_rows(m, carry):
            rows = lax.broadcasted_iota(jnp.int32, (128, n_recv), 0) + m * 128
            hot = jnp.where(rows == at_plane, 1.0, 0.0).astype(BF16)
            for s in range(steps):
                inj[s, p, pl.ds(pl.multiple_of(m * 128, 128), 128), :] = lax.dot_general(
                    hot, b_hi[s], NT, preferred_element_type=F32
                ) + lax.dot_general(hot, b_lo[s], NT, preferred_element_type=F32)
            return carry

        lax.fori_loop(0, size_x * size_y // 128, spread_rows, 0)

    wait_halo(halo_b)

    def stencil(x, carry):
        for t in range(tiles):
            rows = pl.ds(8 * t, 8)
            here = bpad[x + EDGE, pl.ds(TOP + 8 * t, 8), :]
            scale = (0.5 * STEP_SQ) / here
            center = None
            for base, axis in ((1, 0), (7, 1), (13, 2)):
                around = {0: here}
                for k in (-2, -1, 1, 2):
                    if axis == 0:
                        around[k] = bpad[x + EDGE + k, pl.ds(TOP + 8 * t, 8), :]
                    elif axis == 1:
                        around[k] = bpad[x + EDGE, pl.ds(TOP + 8 * t + k, 8), :]
                    else:
                        inside = (lane8 + k >= 0) & (lane8 + k < size_z)
                        around[k] = jnp.where(inside, pltpu.roll(here, (size_z - k) % size_z, 1), 0.0)
                faces = [scale * (around[k] + around[k + 1]) for k in (-2, -1, 0, 1)]
                weights = axis_coefs(faces)
                center = weights[0] if center is None else center + weights[0]
                for at, (k, weight) in enumerate(zip(SHIFTS, weights[1:])):
                    if axis == 2:
                        inside = (lane8 + k >= 0) & (lane8 + k < size_z)
                        weight = jnp.where(inside, weight, 0.0)
                    C[base + at, x, rows, :] = weight
            C[0, x, rows, :] = center
        return carry

    lax.fori_loop(0, size_x, stencil, 0)

    for copy in loads[4:]:
        copy.wait()
    grad_sums = None
    for step in range(steps - 1):
        for kind in range(2):
            wait_halo(halo_w[step + 1, kind])
            wave_step(step, kind)
            send_halo(halo_w[step + 2, kind])

    model_own.wait()
    for copy in model_moves:
        copy.wait()
    blocks = [(a, pl.ds(8 * t, 8)) for a in range(share) for t in range(tiles)]

    def distances(i, carry):
        mine = [mcols[i, a, rows, :] for a, rows in blocks]
        for j in range(particles):
            total = None
            for value, (a, rows) in zip(mine, blocks):
                gap = value - mcols[j, a, rows, :]
                total = gap * gap if total is None else total + gap * gap
            T[i, pl.ds(j, 1), :] = jnp.sum(total, axis=0, keepdims=True)
        return carry

    lax.fori_loop(0, particles, distances, 0)
    pairs = particles * particles
    lane_sums = lax.dot_general(
        jnp.ones((8, size_z), F32),
        T[...].reshape(pairs, size_z),
        NT,
        precision=HIGHEST,
        preferred_element_type=F32,
    )
    gram = jnp.where(row8 == 0, lane_sums[:, :128], lane_sums[:, 128:])
    sum_send_off(gram_dom, "dom", 2, gram)

    step = steps - 1
    wait_halo(halo_w[step + 1, 0])
    grad_sums = wave_step(step, 0)
    grad_moves = column_copies(grad, gcols, 1)
    for copy in grad_moves:
        copy.start()
    grad_own = own_column(grad, gcols, 1)
    grad_own.start()
    norm = jnp.zeros((8, size_z), F32)
    for p in range(parts):
        norm = jnp.where(lane8 % particles == dom * parts + p, jnp.sum(grad_sums[p]), norm)
    sum_send_off(norm_px, "px", 3, norm)
    gram = sum_gather(gram_dom, "dom", 2)
    sum_send_off(gram_px, "px", 0, gram)
    norm = sum_gather(norm_px, "px", 3)
    sum_send_off(norm_py, "py", 4, norm)
    gram = sum_gather(gram_px, "px", 0)
    sum_send_off(gram_py, "py", 1, gram)

    wait_halo(halo_w[step + 1, 1])
    wave_step(step, 1)
    outs = [
        pltpu.make_async_copy(S.at[(state, pl.ds(kind * parts, parts)) + cells], out, out_sem.at[at])
        for at, (state, kind, out) in enumerate(
            ((steps, 0, fb_out), (steps + 1, 0, fa_out), (steps, 1, ab_out), (steps + 1, 1, aa_out))
        )
    ]
    for copy in outs:
        copy.start()
    norm = sum_gather(norm_py, "py", 4)
    sum_send_off(norm_dom, "dom", 5, norm)
    gram = sum_gather(gram_py, "py", 1)

    width = jnp.sum(jnp.where(row8 < 2, gram, 0.0)) / (particles * (particles - 1)) + EPSILON
    weight = jnp.exp(-gram / width)
    square = lax.broadcasted_iota(jnp.int32, (128, 128), 0) == lax.broadcasted_iota(jnp.int32, (128, 128), 1)

    def spread_out_rows(lane, tile):
        for half in range(pairs // 128):
            diagonal = jnp.where(square, tile[half : half + 1, :], 0.0)
            block = jnp.dot(diagonal, jnp.ones((128, size_z), F32), precision=HIGHEST, preferred_element_type=F32)
            KB[lane, pl.ds(half * 128 // particles, 128 // particles)] = block.reshape(
                128 // particles, particles, size_z
            )

    def back_copy(mixed, out, lane, k, target):
        return pltpu.make_async_remote_copy(
            mixed.at[pl.ds(target * parts, parts)],
            out.at[:, pl.ds(dom * share, share)],
            col_send.at[lane, k],
            col_recv.at[lane, k],
            device_id={"dom": target},
            device_id_type=MESH,
        )

    def mix(cols, lane, mixed, out, sem_lane, model):
        def one(k, carry):
            target = lax.rem(dom + k, n_dom)
            for p in range(parts):
                i = target * parts + p
                factors = [KB[lane, i, pl.ds(j, 1), :] for j in range(particles)]
                if model:
                    row_sum = factors[0]
                    for factor in factors[1:]:
                        row_sum = row_sum + factor
                for a, rows in blocks:
                    total = None
                    for j in range(particles):
                        term = factors[j] * cols[j, a, rows, :]
                        total = term if total is None else total + term
                    if model:
                        total = cols[i, a, rows, :] * row_sum - total
                    mixed[i, a, rows, :] = total
            pl.when(k < n_dom)(lambda: back_copy(mixed, out, sem_lane, lax.rem(k, n_dom), target).start())
            return carry

        lax.fori_loop(1, n_dom + 1, one, 0)
        own = pltpu.make_async_copy(
            mixed.at[pl.ds(dom * parts, parts)], out.at[:, pl.ds(dom * share, share)], col_send.at[sem_lane, 0]
        )
        own.start()
        return own

    spread_out_rows(0, weight)
    spread_own = mix(mcols, 0, mix_m, spread_out, 2, True)

    norm = sum_gather(norm_dom, "dom", 5)
    scale = 1.0 / jnp.sqrt(norm / float(total_x * total_y * size_z) + EPSILON)
    spread_out_rows(1, weight * scale)
    grad_own.wait()
    for copy in grad_moves:
        copy.wait()
    drift_own = mix(gcols, 1, mix_g, drift_out, 3, False)

    for copy in outs:
        copy.wait()
    spread_own.wait()
    drift_own.wait()
    for k in range(1, n_dom):
        back_copy(mix_m, spread_out, 2, k, peer("dom", k)).wait()
    for k in range(1, n_dom):
        back_copy(mix_g, drift_out, 3, k, peer("dom", k)).wait()


def on_device(counts, *args):
    velocity, wavelet, receivers = args[0], args[7], args[8]
    parts, size_x, size_y, size_z = velocity.shape
    steps, n_recv = wavelet.shape[1], receivers.shape[1]
    n_px, n_py, n_dom = counts
    particles = parts * n_dom
    share = size_x // n_dom
    pad_x, pad_y = size_x + 2 * EDGE, size_y + 2 * TOP
    whole = (parts, size_x, size_y, size_z)
    cols = (particles, share, size_y, size_z)
    most = max(counts)
    anywhere = pl.BlockSpec(memory_space=pl.ANY)
    vmem = pl.BlockSpec(memory_space=pltpu.VMEM)
    smem = pl.BlockSpec(memory_space=pltpu.SMEM)
    dma = pltpu.SemaphoreType.DMA
    return pl.pallas_call(
        functools.partial(kernel, counts),
        out_shape=[jax.ShapeDtypeStruct(whole, F32)] * 6,
        in_specs=[anywhere] * 6 + [smem, smem, vmem, vmem, smem],
        out_specs=[anywhere] * 6,
        scratch_shapes=[
            pltpu.VMEM((steps + 2, 2 * parts, pad_x, pad_y, size_z), F32),
            pltpu.VMEM(whole, F32),
            pltpu.VMEM((pad_x, pad_y, size_z), F32),
            pltpu.VMEM((19, size_x, size_y, size_z), F32),
            pltpu.VMEM((size_x, size_y, size_z), F32),
            pltpu.VMEM(whole, F32),
            pltpu.VMEM((steps, parts, size_x * size_y, size_z), F32),
            pltpu.VMEM((steps, size_z, n_recv), BF16),
            pltpu.VMEM((steps, size_z, n_recv), BF16),
            pltpu.VMEM(whole, F32),
            pltpu.VMEM(cols, F32),
            pltpu.VMEM(cols, F32),
            pltpu.VMEM(cols, F32),
            pltpu.VMEM(cols, F32),
            pltpu.VMEM((particles, particles, size_z), F32),
            pltpu.VMEM((2, particles, particles, size_z), F32),
            pltpu.VMEM((n_px, 8, size_z), F32),
            pltpu.VMEM((n_py, 8, size_z), F32),
            pltpu.VMEM((n_dom, 8, size_z), F32),
            pltpu.VMEM((n_px, 8, size_z), F32),
            pltpu.VMEM((n_py, 8, size_z), F32),
            pltpu.VMEM((n_dom, 8, size_z), F32),
            dma((6,)),
            dma((1 + 2 * steps, 4)),
            dma((1 + 2 * steps, 4)),
            dma((4, n_dom)),
            dma((4, n_dom)),
            dma((6, most)),
            dma((6, most)),
            dma((4,)),
        ],
        compiler_params=pltpu.CompilerParams(collective_id=0, has_side_effects=True, vmem_limit_bytes=60 * 1024 * 1024),
    )(*args)


def solution(mesh):
    counts = (mesh.shape["px"], mesh.shape["py"], mesh.shape["dom"])
    field = P("dom", "px", "py", None)
    return jax.shard_map(
        functools.partial(on_device, counts),
        mesh=mesh,
        in_specs=(
            field,
            P("px", "py", None),
            field,
            field,
            field,
            field,
            P("dom"),
            P("dom", None),
            P("dom", None),
            P("dom", None, None),
            P(),
        ),
        out_specs=(field,) * 6,
        check_vma=False,
    )
```

time: 339 us -> 85.4 us (0.25)
  blocking collectives: 168 us -> 0 us
  Pallas kernels: 0 us -> 75.3 us
  starting transfers between devices: 68.8 us -> 0 us
  other arithmetic: 35.5 us -> 0 us
  waiting for transfers between devices: 34.7 us -> 0 us
  matrix products: 10.2 us -> 0 us
  local copies, waits for them, and re-layouts: 15.2 us -> 9.01 us
  between operations: 5.78 us -> 0.66 us
    psum x2 -> x0, blocking collectives: 149 us -> none  [the longest x1 79.6 us: on_device(): gram_total = lax.psum(gram_part, ('px', 'py', 'dom'))]
    pallas_call x0 -> x1, Pallas kernels: none -> 75.3 us  [on_device(): pl.pallas_call(functools.partial(kernel, counts), out_shape=[jax.ShapeDty...]
    ppermute x16 -> x0, starting transfers between devices: 52.2 us -> none  [the longest x8 34.8 us: with_halo(): lax.ppermute(tail, axis, [(i, (i + 1) % count) for i in range(ends)])]
    all_to_all x3 -> x0, waiting for transfers between devices: 23.7 us -> none  [the longest x1 15.1 us: on_device(): lax.all_to_all(mixed_grad, 'dom', split_axis=0, concat_axis=1, tiled=True)]
    all_to_all x1 -> x0, blocking collectives: 19.1 us -> none  [on_device(): lax.all_to_all(flat_grad, 'dom', split_axis=1, concat_axis=0, tiled=True)]
    all_to_all x3 -> x0, starting transfers between devices: 16.6 us -> none  [the longest x1 7.67 us: on_device(): lax.all_to_all(flat_model, 'dom', split_axis=1, concat_axis=0, tiled=True)]
    mul x17 -> x0, other arithmetic: 15.1 us -> none  [the longest x9 13.4 us: axis_term(): flux_face = half_buoy * slope_face]
    ppermute x16 -> x0, waiting for transfers between devices: 11 us -> none  [the longest x8 7.5 us: with_halo(): lax.ppermute(tail, axis, [(i, (i + 1) % count) for i in range(ends)])]
  transfers between devices with their start and end apart: 19 -> 0, of which waited for: 8 -> 0; matrix products, arithmetic and copies ran while one was open for 10% -> 0% of each run, Pallas kernels for 0% -> 0%
where the time goes in v1:
time: 85.4 us; the launch traced here: 84.9 us
  Pallas kernels  75.3 us (88%)
  local copies, waits for them, and re-layouts  9.01 us (11%)
    pallas_call x1, Pallas kernels, on_device(): pl.pallas_call(functools.partial(kernel, counts), out_shape=[jax.ShapeDty...  75.3 us
    unnamed x17, local copies, waits for them, and re-layouts  9.01 us

profile of v1, /device:TPU:1, one launch (start us, length us, event | category | flops | bytes accessed | tf_op | source)
XLA Modules:
  0.0 84.9 jit_solution(9240799306862575969)
XLA Ops:
  0.6 1.4 %copy.17.misfit = f32[2,3,1024]{2,1,0:T(4,128)} copy(f32[2,3,1024]{2,0,1:T(2,128)} %param.20) | data formatting | bytes 49152 | tf_op args[9]
  2.0 75.3 %shard_map.154 = (f32[2,16,32,128]{3,2,1,0:T(8,128)}, f32[2,16,32,128]{3,2,1,0:T(8,128)}, f32[2,16,32,128]{3,2,1,0:T(8,128)}, f32[2,16,32,128]{3,2,1,0:T(8,128)}...) custom-call(f32[2,16,32,128]{3,2,1,0:T(8,128)} %vel_in.1, f32[16,32,128]{2,1,0:T(8,128)} %buoy_in.1, ...), custom_call_target="tpu_custom_call" | custom-call | tf_op jit(solution)/shard_map/pallas_call | solution.py:546
  77.3 0.0 copy-start.4
  77.3 1.9 %copy.24 = f32[2,16,32,128]{3,2,1,0:T(8,128)} copy(f32[2,16,32,128]{3,2,1,0:T(8,128)} %get-tuple-element.12) | data formatting | bytes 1048576
  79.2 0.0 copy-done.4
  79.2 0.0 copy-start.3
  79.2 0.8 copy.25
  80.0 0.4 copy-done.3
  80.4 0.0 copy-start.2
  80.4 0.8 copy.26
  81.2 0.4 copy-done.2
  81.7 0.0 copy-start.1
  81.7 0.8 copy.27
  82.5 0.4 copy-done.1
  82.9 0.0 copy-start
  82.9 0.8 copy.28
  83.7 0.4 copy-done
  84.1 0.8 copy.29
Async XLA Ops:
  77.3 1.9 %copy-start.4 = (f32[2,16,32,128]{3,2,1,0:T(8,128)S(1)}, f32[2,16,32,128]{3,2,1,0:T(8,128)}, u32[]{:S(2)}) copy-start(f32[2,16,32,128]{3,2,1,0:T(8,128)} %get-tuple-element.13) | copy-start | bytes 1572868
  79.2 1.2 %copy-start.3 = (f32[2,16,32,128]{3,2,1,0:T(8,128)S(1)}, f32[2,16,32,128]{3,2,1,0:T(8,128)}, u32[]{:S(2)}) copy-start(f32[2,16,32,128]{3,2,1,0:T(8,128)} %get-tuple-element.14) | copy-start | bytes 1572868
  80.4 1.2 %copy-start.2 = (f32[2,16,32,128]{3,2,1,0:T(8,128)S(1)}, f32[2,16,32,128]{3,2,1,0:T(8,128)}, u32[]{:S(2)}) copy-start(f32[2,16,32,128]{3,2,1,0:T(8,128)} %get-tuple-element.15) | copy-start | bytes 1572868
  81.7 1.2 %copy-start.1 = (f32[2,16,32,128]{3,2,1,0:T(8,128)S(1)}, f32[2,16,32,128]{3,2,1,0:T(8,128)}, u32[]{:S(2)}) copy-start(f32[2,16,32,128]{3,2,1,0:T(8,128)} %get-tuple-element.16) | copy-start | bytes 1572868
  82.9 1.2 %copy-start = (f32[2,16,32,128]{3,2,1,0:T(8,128)S(1)}, f32[2,16,32,128]{3,2,1,0:T(8,128)}, u32[]{:S(2)}) copy-start(f32[2,16,32,128]{3,2,1,0:T(8,128)} %get-tuple-element.17) | copy-start | bytes 1572868

commit v2 on v1

--- a/solution.py
+++ b/solution.py
@@ -72,8 +72,11 @@
     damp,
     src_hot,
     inj,
-    b_hi,
-    b_lo,
+    b_parts,
+    hot,
+    fade_speed,
+    grad_scale,
+    base,
     grad,
     mcols,
     gcols,
@@ -94,7 +97,6 @@
     col_recv,
     sum_send,
     sum_recv,
-    out_sem,
 ):
     n_px, n_py, n_dom = counts
     parts, size_x, size_y, size_z = vel.shape
@@ -249,53 +251,73 @@
             value = value + buffer[k]
         return value
 
-    def wave_step(step, kind):
+    def pre_step(step, kind):
+        now, before = step + 1, step
+
+        def plane(x, carry):
+            for t in range(tiles):
+                rows, wide = pl.ds(8 * t, 8), pl.ds(TOP + 8 * t, 8)
+                weights = [C[k, x, rows, :] for k in (0, 13, 14, 15, 16, 17, 18)]
+                fade = damp[x, rows, :]
+                for p in range(parts):
+                    f = kind * parts + p
+                    here = S[now, f, x + EDGE, wide, :]
+                    old = S[before, f, x + EDGE, wide, :]
+                    lap = weights[0] * here
+                    for k, weight in zip(SHIFTS, weights[1:]):
+                        lap = lap + weight * pltpu.roll(here, (size_z - k) % size_z, 1)
+                    if kind == 0:
+                        add = src_hot[p, x, rows, :] * (STEP_SQ * wavelet[p, step])
+                    else:
+                        add = inj[step, p, pl.ds(pl.multiple_of(x * size_y, size_y) + 8 * t, 8), :]
+                    base[kind, p, x, rows, :] = fade_speed[p, x, rows, :] * lap + fade * ((here + here) - old + add)
+                    if kind == 0 and step > 0:
+                        older = S[before - 1, f, x + EDGE, wide, :]
+                        part = S[before, parts + p, x + EDGE, wide, :] * ((here - (old + old)) + older)
+                        if step > 1:
+                            part = part + grad[p, x, rows, :]
+                        grad[p, x, rows, :] = part
+            return carry
+
+        lax.fori_loop(0, size_x, plane, 0, unroll=2)
+
+    def post_step(step, kind):
         now, before, later = step + 1, step, step + 2
         last = step == steps - 1
 
         def plane(x, carry):
             sums = list(carry)
             for t in range(tiles):
-                rows = pl.ds(8 * t, 8)
-                weights = [C[k, x, rows, :] for k in range(19)]
-                fade = damp[x, rows, :]
+                rows, wide = pl.ds(8 * t, 8), pl.ds(TOP + 8 * t, 8)
+                weights = [C[1 + k, x, rows, :] for k in range(12)]
                 for p in range(parts):
                     f = kind * parts + p
-                    here = S[now, f, x + EDGE, pl.ds(TOP + 8 * t, 8), :]
-                    along_x = [S[now, f, x + EDGE + k, pl.ds(TOP + 8 * t, 8), :] for k in SHIFTS]
-                    along_y = [S[now, f, x + EDGE, pl.ds(TOP + 8 * t + k, 8), :] for k in SHIFTS]
-                    along_z = [pltpu.roll(here, (size_z - k) % size_z, 1) for k in SHIFTS]
-                    terms = [weights[0] * here]
-                    for base, values in ((1, along_x), (7, along_y), (13, along_z)):
-                        part = None
-                        for k, value in enumerate(values):
-                            term = weights[base + k] * value
-                            part = term if part is None else part + term
-                        terms.append(part)
-                    lap = (terms[0] + terms[1]) + (terms[2] + terms[3])
-                    speed = vel[p, x, rows, :]
-                    old = S[before, f, x + EDGE, pl.ds(TOP + 8 * t, 8), :]
-                    bend = old - 2.0 * here
-                    new = (speed * speed) * lap - bend
-                    if kind == 0:
-                        new = new + src_hot[p, x, rows, :] * (STEP_SQ * wavelet[p, step])
-                    else:
-                        new = new + inj[step, p, pl.ds(pl.multiple_of(x * size_y, size_y) + 8 * t, 8), :]
-                    new = fade * new
-                    S[later, f, x + EDGE, pl.ds(TOP + 8 * t, 8), :] = new
-                    if kind == 0:
-                        other = S[now, parts + p, x + EDGE, pl.ds(TOP + 8 * t, 8), :]
-                        add = other * (new + bend)
+                    lap = None
+                    for k, weight in zip(SHIFTS, weights[:6]):
+                        term = weight * S[now, f, x + EDGE + k, wide, :]
+                        lap = term if lap is None else lap + term
+                    for k, weight in zip(SHIFTS, weights[6:]):
+                        lap = lap + weight * S[now, f, x + EDGE, pl.ds(TOP + 8 * t + k, 8), :]
+                    new = base[kind, p, x, rows, :] + fade_speed[p, x, rows, :] * lap
+                    if not last:
+                        S[later, f, x + EDGE, wide, :] = new
+                    if step >= steps - 2:
+                        results[kind][step - steps + 2][p, x, rows, :] = new
+                    if kind == 0 and last:
+                        here = S[now, f, x + EDGE, wide, :]
+                        bend = (new - (here + here)) + S[before, f, x + EDGE, wide, :]
+                        part = S[now, parts + p, x + EDGE, wide, :] * bend
                         if step > 0:
-                            add = add + grad[p, x, rows, :]
-                        if last:
-                            add = add * (-2.0 / (speed * speed * speed))
-                            sums[p] = sums[p] + add * add
-                        grad[p, x, rows, :] = add
+                            part = part + grad[p, x, rows, :]
+                        part = part * grad_scale[p, x, rows, :]
+                        sums[p] = sums[p] + part * part
+                        grad[p, x, rows, :] = part
             return tuple(sums)
 
         start = tuple(jnp.zeros((8, size_z), F32) for _ in range(parts)) if kind == 0 and last else ()
-        return lax.fori_loop(0, size_x, plane, start)
+        return lax.fori_loop(0, size_x, plane, start, unroll=2)
+
+    results = ((fb_out, fa_out), (ab_out, aa_out))
 
     for copy in loads[:4]:
         copy.wait()
@@ -325,6 +347,10 @@
             damp[x, rows, :] = jnp.exp(-(fade_x + fade_yz[t]))
             flat = (at_x * total_y + (row8 + (8 * t + base_y))) * size_z + lane8
             for p in range(parts):
+                speed = vel[p, x, rows, :]
+                square = speed * speed
+                fade_speed[p, x, rows, :] = damp[x, rows, :] * square
+                grad_scale[p, x, rows, :] = -2.0 / (square * speed)
                 src_hot[p, x, rows, :] = jnp.where(flat == sources[p], 1.0, 0.0)
         return carry
 
@@ -332,30 +358,44 @@
 
     z_bits, y_bits = size_z.bit_length() - 1, total_y.bit_length() - 1
     n_recv = receivers.shape[1]
-    for p in range(parts):
+    row16 = lax.broadcasted_iota(jnp.int32, (16, n_recv), 0)
+
+    def inject(p):
         index = receivers[pl.ds(p, 1), :]
         local_x = (index >> (z_bits + y_bits)) - base_x
         local_y = ((index >> z_bits) & (total_y - 1)) - base_y
-        depth = index & (size_z - 1)
         inside = (local_x >= 0) & (local_x < size_x) & (local_y >= 0) & (local_y < size_y)
-        at_plane = jnp.where(inside, local_x * size_y + local_y, -1)
-        hit = lax.broadcasted_iota(jnp.int32, (size_z, n_recv), 0) == depth
+        at_plane = jnp.where(inside, local_x * size_y + local_y, -1) - row16
+        depth = (index & (size_z - 1)) - row16
+        amounts = []
         for s in range(steps):
-            amount = STEP_SQ * misfit[p, pl.ds(s, 1), :]
+            amount = STEP_SQ * misfit[s, pl.ds(p, 1), :]
             high = amount.astype(BF16).astype(F32)
-            b_hi[s] = jnp.where(hit, high, 0.0).astype(BF16)
-            b_lo[s] = jnp.where(hit, amount - high, 0.0).astype(BF16)
-
-        def spread_rows(m, carry):
-            rows = lax.broadcasted_iota(jnp.int32, (128, n_recv), 0) + m * 128
-            hot = jnp.where(rows == at_plane, 1.0, 0.0).astype(BF16)
-            for s in range(steps):
-                inj[s, p, pl.ds(pl.multiple_of(m * 128, 128), 128), :] = lax.dot_general(
-                    hot, b_hi[s], NT, preferred_element_type=F32
-                ) + lax.dot_general(hot, b_lo[s], NT, preferred_element_type=F32)
+            amounts += [high, amount - high]
+
+        def depths(m, carry):
+            hit = depth == m * 16
+            for k, amount in enumerate(amounts):
+                b_parts[k, pl.ds(pl.multiple_of(m * 16, 16), 16), :] = jnp.where(hit, amount, 0.0).astype(BF16)
             return carry
 
-        lax.fori_loop(0, size_x * size_y // 128, spread_rows, 0)
+        lax.fori_loop(0, size_z // 16, depths, 0)
+
+        def planes(m, carry):
+            hot[pl.ds(pl.multiple_of(m * 16, 16), 16), :] = jnp.where(at_plane == m * 16, 1.0, 0.0).astype(BF16)
+            return carry
+
+        lax.fori_loop(0, size_x * size_y // 16, planes, 0, unroll=2)
+        for s in range(steps):
+            both = lax.dot_general(
+                hot[...],
+                b_parts[pl.ds(2 * s, 2)].reshape(2 * size_z, n_recv),
+                NT,
+                preferred_element_type=F32,
+            )
+            inj[s, p] = both[:, :size_z] + both[:, size_z:]
+
+    inject(0)
 
     wait_halo(halo_b)
 
@@ -390,12 +430,21 @@
 
     for copy in loads[4:]:
         copy.wait()
-    grad_sums = None
-    for step in range(steps - 1):
-        for kind in range(2):
-            wait_halo(halo_w[step + 1, kind])
-            wave_step(step, kind)
-            send_halo(halo_w[step + 2, kind])
+    pre_step(0, 0)
+    wait_halo(halo_w[1, 0])
+    post_step(0, 0)
+    send_halo(halo_w[2, 0])
+    for p in range(1, parts):
+        inject(p)
+    pre_step(0, 1)
+    wait_halo(halo_w[1, 1])
+    post_step(0, 1)
+    send_halo(halo_w[2, 1])
+    pre_step(1, 0)
+    wait_halo(halo_w[2, 0])
+    post_step(1, 0)
+    send_halo(halo_w[3, 0])
+    pre_step(2, 0)
 
     model_own.wait()
     for copy in model_moves:
@@ -423,10 +472,13 @@
     )
     gram = jnp.where(row8 == 0, lane_sums[:, :128], lane_sums[:, 128:])
     sum_send_off(gram_dom, "dom", 2, gram)
-
-    step = steps - 1
-    wait_halo(halo_w[step + 1, 0])
-    grad_sums = wave_step(step, 0)
+    pre_step(1, 1)
+    wait_halo(halo_w[2, 1])
+    post_step(1, 1)
+    send_halo(halo_w[3, 1])
+
+    wait_halo(halo_w[3, 0])
+    grad_sums = post_step(2, 0)
     grad_moves = column_copies(grad, gcols, 1)
     for copy in grad_moves:
         copy.start()
@@ -443,16 +495,9 @@
     gram = sum_gather(gram_px, "px", 0)
     sum_send_off(gram_py, "py", 1, gram)
 
-    wait_halo(halo_w[step + 1, 1])
-    wave_step(step, 1)
-    outs = [
-        pltpu.make_async_copy(S.at[(state, pl.ds(kind * parts, parts)) + cells], out, out_sem.at[at])
-        for at, (state, kind, out) in enumerate(
-            ((steps, 0, fb_out), (steps + 1, 0, fa_out), (steps, 1, ab_out), (steps + 1, 1, aa_out))
-        )
-    ]
-    for copy in outs:
-        copy.start()
+    pre_step(2, 1)
+    wait_halo(halo_w[3, 1])
+    post_step(2, 1)
     norm = sum_gather(norm_py, "py", 4)
     sum_send_off(norm_dom, "dom", 5, norm)
     gram = sum_gather(gram_py, "py", 1)
@@ -518,14 +563,21 @@
         copy.wait()
     drift_own = mix(gcols, 1, mix_g, drift_out, 3, False)
 
-    for copy in outs:
-        copy.wait()
     spread_own.wait()
     drift_own.wait()
     for k in range(1, n_dom):
         back_copy(mix_m, spread_out, 2, k, peer("dom", k)).wait()
     for k in range(1, n_dom):
         back_copy(mix_g, drift_out, 3, k, peer("dom", k)).wait()
+
+
+def put_out(*refs):
+    sem = refs[-1]
+    copies = [pltpu.make_async_copy(refs[k], refs[6 + k], sem.at[k]) for k in range(6)]
+    for copy in copies:
+        copy.start()
+    for copy in copies:
+        copy.wait()
 
 
 def on_device(counts, *args):
@@ -539,25 +591,29 @@
     whole = (parts, size_x, size_y, size_z)
     cols = (particles, share, size_y, size_z)
     most = max(counts)
-    anywhere = pl.BlockSpec(memory_space=pl.ANY)
+    hbm = pl.BlockSpec(memory_space=pltpu.HBM)
     vmem = pl.BlockSpec(memory_space=pltpu.VMEM)
     smem = pl.BlockSpec(memory_space=pltpu.SMEM)
     dma = pltpu.SemaphoreType.DMA
-    return pl.pallas_call(
+    args = args[:9] + (jnp.transpose(args[9], (1, 0, 2)), args[10])
+    results = pl.pallas_call(
         functools.partial(kernel, counts),
-        out_shape=[jax.ShapeDtypeStruct(whole, F32)] * 6,
-        in_specs=[anywhere] * 6 + [smem, smem, vmem, vmem, smem],
-        out_specs=[anywhere] * 6,
+        out_shape=[pltpu.VMEM(whole, F32)] * 6,
+        in_specs=[hbm] * 6 + [smem, smem, vmem, vmem, smem],
+        out_specs=[vmem] * 6,
         scratch_shapes=[
-            pltpu.VMEM((steps + 2, 2 * parts, pad_x, pad_y, size_z), F32),
+            pltpu.VMEM((steps + 1, 2 * parts, pad_x, pad_y, size_z), F32),
             pltpu.VMEM(whole, F32),
             pltpu.VMEM((pad_x, pad_y, size_z), F32),
             pltpu.VMEM((19, size_x, size_y, size_z), F32),
             pltpu.VMEM((size_x, size_y, size_z), F32),
             pltpu.VMEM(whole, F32),
             pltpu.VMEM((steps, parts, size_x * size_y, size_z), F32),
-            pltpu.VMEM((steps, size_z, n_recv), BF16),
-            pltpu.VMEM((steps, size_z, n_recv), BF16),
+            pltpu.VMEM((2 * steps, size_z, n_recv), BF16),
+            pltpu.VMEM((size_x * size_y, n_recv), BF16),
+            pltpu.VMEM(whole, F32),
+            pltpu.VMEM(whole, F32),
+            pltpu.VMEM((2,) + whole, F32),
             pltpu.VMEM(whole, F32),
             pltpu.VMEM(cols, F32),
             pltpu.VMEM(cols, F32),
@@ -578,10 +634,17 @@
             dma((4, n_dom)),
             dma((6, most)),
             dma((6, most)),
-            dma((4,)),
         ],
-        compiler_params=pltpu.CompilerParams(collective_id=0, has_side_effects=True, vmem_limit_bytes=60 * 1024 * 1024),
-    )(*args)
+        compiler_params=pltpu.CompilerParams(collective_id=0, has_side_effects=True, vmem_limit_bytes=40 * 1024 * 1024),
+    )(*[pltpu.with_memory_space_constraint(arg, pltpu.HBM) for arg in args])
+    results = [pltpu.with_memory_space_constraint(result, pltpu.VMEM) for result in results]
+    return pl.pallas_call(
+        put_out,
+        out_shape=[jax.ShapeDtypeStruct(whole, F32)] * 6,
+        in_specs=[vmem] * 6,
+        out_specs=[hbm] * 6,
+        scratch_shapes=[dma((6,))],
+    )(*results)
 
 
 def solution(mesh):

time: 85.4 us -> 74.2 us (0.87)
  local copies, waits for them, and re-layouts: 9.01 us -> 0 us
  Pallas kernels: 75.3 us -> 73.4 us
    unnamed x17 -> x0, local copies, waits for them, and re-layouts: 9.01 us -> none
    pallas_call x1 -> x2, Pallas kernels: 75.3 us -> 73.4 us  [the longest x1 71.7 us: on_device(): pl.pallas_call(functools.partial(kernel, counts), out_shape=[pltpu.VMEM(w...]
where the time goes in v2:
time: 74.2 us; the launch traced here: 74 us
  Pallas kernels  73.4 us (99%)
    pallas_call x1, Pallas kernels, on_device(): pl.pallas_call(functools.partial(kernel, counts), out_shape=[pltpu.VMEM(w...  71.7 us
    pallas_call x1, Pallas kernels, on_device(): pl.pallas_call(put_out, out_shape=[jax.ShapeDtypeStruct(whole, F32)] * 6,...  1.71 us

profile of v2, /device:TPU:1, one launch (start us, length us, event | category | flops | bytes accessed | tf_op | source)
XLA Modules:
  0.0 74.0 jit_solution(4650812515113472270)
XLA Ops:
  0.6 71.7 %shard_map.154 = (f32[2,16,32,128]{3,2,1,0:T(8,128)S(1)}, f32[2,16,32,128]{3,2,1,0:T(8,128)S(1)}, f32[2,16,32,128]{3,2,1,0:T(8,128)S(1)}, f32[2,16,32,128]{3,2,1...) custom-call(f32[2,16,32,128]{3,2,1,0:T(8,128)} %vel_in.1, f32[16,32,128]{2,1,0:T(8,128)} %buoy_in.1, ...), custom_call_target="tpu_custom_call" | custom-call | tf_op jit(solution)/shard_map/pallas_call | solution.py:599
  72.3 1.7 %shard_map.155 = (f32[2,16,32,128]{3,2,1,0:T(8,128)}, f32[2,16,32,128]{3,2,1,0:T(8,128)}, f32[2,16,32,128]{3,2,1,0:T(8,128)}, f32[2,16,32,128]{3,2,1,0:T(8,128)}...) custom-call(f32[2,16,32,128]{3,2,1,0:T(8,128)S(1)} %get-tuple-element.12.refs_0_, ...), custom_call_target="tpu_custom_call" | custom-call | tf_op jit(solution)/shard_map/pallas_call | solution.py:641

commit v3 on v2

--- a/solution.py
+++ b/solution.py
@@ -54,17 +54,22 @@
     fn_in,
     ap_in,
     an_in,
-    sources,
-    wavelet,
-    receivers,
-    misfit,
-    sponge,
+    sources_in,
+    wavelet_in,
+    receivers_in,
+    misfit_in,
+    sponge_in,
     fb_out,
     fa_out,
     ab_out,
     aa_out,
     drift_out,
     spread_out,
+    sources,
+    wavelet,
+    receivers,
+    misfit,
+    sponge,
     S,
     vel,
     bpad,
@@ -128,6 +133,15 @@
         pltpu.make_async_copy(fp_in, S.at[(0, pl.ds(0, parts)) + cells], load_sem.at[4]),
         pltpu.make_async_copy(ap_in, S.at[(0, pl.ds(parts, parts)) + cells], load_sem.at[5]),
     ]
+    small = (
+        (sources_in, sources),
+        (wavelet_in, wavelet),
+        (receivers_in, receivers),
+        (misfit_in, misfit),
+        (sponge_in, sponge),
+    )
+    for at, (src, dst) in enumerate(small):
+        loads.append(pltpu.make_async_copy(src, dst, load_sem.at[6 + at]))
     for copy in loads:
         copy.start()
 
@@ -289,14 +303,13 @@
             sums = list(carry)
             for t in range(tiles):
                 rows, wide = pl.ds(8 * t, 8), pl.ds(TOP + 8 * t, 8)
-                weights = [C[1 + k, x, rows, :] for k in range(12)]
+                weights = [C[1 + k, x, rows, :] for k in range(12)] + [C[19, x, rows, :]]
                 for p in range(parts):
                     f = kind * parts + p
-                    lap = None
+                    lap = weights[12] * S[now, f, x + EDGE, wide, :]
                     for k, weight in zip(SHIFTS, weights[:6]):
-                        term = weight * S[now, f, x + EDGE + k, wide, :]
-                        lap = term if lap is None else lap + term
-                    for k, weight in zip(SHIFTS, weights[6:]):
+                        lap = lap + weight * S[now, f, x + EDGE + k, wide, :]
+                    for k, weight in zip(SHIFTS, weights[6:12]):
                         lap = lap + weight * S[now, f, x + EDGE, pl.ds(TOP + 8 * t + k, 8), :]
                     new = base[kind, p, x, rows, :] + fade_speed[p, x, rows, :] * lap
                     if not last:
@@ -331,6 +344,9 @@
     model_own = own_column(vel, mcols, 0)
     model_own.start()
 
+    for copy in loads[6:]:
+        copy.wait()
+
     widths = [sponge[k].astype(F32) for k in range(6)]
     base_x, base_y = px * size_x, py * size_y
     fade_yz = [
@@ -395,42 +411,46 @@
             )
             inj[s, p] = both[:, :size_z] + both[:, size_z:]
 
-    inject(0)
-
-    wait_halo(halo_b)
-
-    def stencil(x, carry):
+
+    def face_weights(around, scale):
+        return axis_coefs([scale * (around[k] + around[k + 1]) for k in (-2, -1, 0, 1)])
+
+    def stencil_z(x, carry):
+        for t in range(tiles):
+            rows = pl.ds(8 * t, 8)
+            here = bpad[x + EDGE, pl.ds(TOP + 8 * t, 8), :]
+            around = {0: here}
+            for k in (-2, -1, 1, 2):
+                around[k] = jnp.where(within[k], pltpu.roll(here, (size_z - k) % size_z, 1), 0.0)
+            weights = face_weights(around, (0.5 * STEP_SQ) / here)
+            C[0, x, rows, :] = weights[0]
+            for at, (k, weight) in enumerate(zip(SHIFTS, weights[1:])):
+                C[13 + at, x, rows, :] = jnp.where(within[k], weight, 0.0)
+        return carry
+
+    def stencil_xy(x, carry):
         for t in range(tiles):
             rows = pl.ds(8 * t, 8)
             here = bpad[x + EDGE, pl.ds(TOP + 8 * t, 8), :]
             scale = (0.5 * STEP_SQ) / here
-            center = None
-            for base, axis in ((1, 0), (7, 1), (13, 2)):
-                around = {0: here}
-                for k in (-2, -1, 1, 2):
-                    if axis == 0:
-                        around[k] = bpad[x + EDGE + k, pl.ds(TOP + 8 * t, 8), :]
-                    elif axis == 1:
-                        around[k] = bpad[x + EDGE, pl.ds(TOP + 8 * t + k, 8), :]
-                    else:
-                        inside = (lane8 + k >= 0) & (lane8 + k < size_z)
-                        around[k] = jnp.where(inside, pltpu.roll(here, (size_z - k) % size_z, 1), 0.0)
-                faces = [scale * (around[k] + around[k + 1]) for k in (-2, -1, 0, 1)]
-                weights = axis_coefs(faces)
-                center = weights[0] if center is None else center + weights[0]
-                for at, (k, weight) in enumerate(zip(SHIFTS, weights[1:])):
-                    if axis == 2:
-                        inside = (lane8 + k >= 0) & (lane8 + k < size_z)
-                        weight = jnp.where(inside, weight, 0.0)
-                    C[base + at, x, rows, :] = weight
-            C[0, x, rows, :] = center
+            at_x = {k: bpad[x + EDGE + k, pl.ds(TOP + 8 * t, 8), :] for k in range(-2, 3)}
+            at_y = {k: bpad[x + EDGE, pl.ds(TOP + 8 * t + k, 8), :] for k in range(-2, 3)}
+            along_x, along_y = face_weights(at_x, scale), face_weights(at_y, scale)
+            C[19, x, rows, :] = along_x[0] + along_y[0]
+            for at in range(6):
+                C[1 + at, x, rows, :] = along_x[1 + at]
+                C[7 + at, x, rows, :] = along_y[1 + at]
         return carry
 
-    lax.fori_loop(0, size_x, stencil, 0)
-
-    for copy in loads[4:]:
+    within = {k: (lane8 + k >= 0) & (lane8 + k < size_z) for k in SHIFTS}
+    lax.fori_loop(0, size_x, stencil_z, 0)
+    for copy in loads[4:6]:
         copy.wait()
     pre_step(0, 0)
+    inject(0)
+    wait_halo(halo_b)
+    lax.fori_loop(0, size_x, stencil_xy, 0)
+
     wait_halo(halo_w[1, 0])
     post_step(0, 0)
     send_halo(halo_w[2, 0])
@@ -451,14 +471,18 @@
         copy.wait()
     blocks = [(a, pl.ds(8 * t, 8)) for a in range(share) for t in range(tiles)]
 
+    half = particles // 2
+    T[...] = jnp.zeros_like(T)
+
     def distances(i, carry):
         mine = [mcols[i, a, rows, :] for a, rows in blocks]
-        for j in range(particles):
+        for k in range(1, half + 1):
+            j = lax.rem(i + k, particles)
             total = None
             for value, (a, rows) in zip(mine, blocks):
                 gap = value - mcols[j, a, rows, :]
                 total = gap * gap if total is None else total + gap * gap
-            T[i, pl.ds(j, 1), :] = jnp.sum(total, axis=0, keepdims=True)
+            T[i, pl.ds(k, 1), :] = jnp.sum(total, axis=0, keepdims=True)
         return carry
 
     lax.fori_loop(0, particles, distances, 0)
@@ -502,17 +526,15 @@
     sum_send_off(norm_dom, "dom", 5, norm)
     gram = sum_gather(gram_py, "py", 1)
 
-    width = jnp.sum(jnp.where(row8 < 2, gram, 0.0)) / (particles * (particles - 1)) + EPSILON
+    twice = jnp.where(lane8 % particles == half, 1.0, 2.0)
+    width = jnp.sum(jnp.where(row8 < 2, gram * twice, 0.0)) / (particles * (particles - 1)) + EPSILON
     weight = jnp.exp(-gram / width)
     square = lax.broadcasted_iota(jnp.int32, (128, 128), 0) == lax.broadcasted_iota(jnp.int32, (128, 128), 1)
 
-    def spread_out_rows(lane, tile):
-        for half in range(pairs // 128):
-            diagonal = jnp.where(square, tile[half : half + 1, :], 0.0)
-            block = jnp.dot(diagonal, jnp.ones((128, size_z), F32), precision=HIGHEST, preferred_element_type=F32)
-            KB[lane, pl.ds(half * 128 // particles, 128 // particles)] = block.reshape(
-                128 // particles, particles, size_z
-            )
+    def rows_of(row):
+        return jnp.dot(
+            jnp.where(square, row, 0.0), jnp.ones((128, size_z), F32), precision=HIGHEST, preferred_element_type=F32
+        )
 
     def back_copy(mixed, out, lane, k, target):
         return pltpu.make_async_remote_copy(
@@ -524,20 +546,22 @@
             device_id_type=MESH,
         )
 
-    def mix(cols, lane, mixed, out, sem_lane, model):
+    def mix(cols, mixed, out, sem_lane, model):
         def one(k, carry):
             target = lax.rem(dom + k, n_dom)
             for p in range(parts):
                 i = target * parts + p
-                factors = [KB[lane, i, pl.ds(j, 1), :] for j in range(particles)]
+                others = [lax.rem(i + k, particles) for k in range(particles)]
+                factors = [KB[i, pl.ds(k, 1), :] for k in range(half + 1)]
+                factors += [KB[others[k], pl.ds(particles - k, 1), :] for k in range(half + 1, particles)]
                 if model:
                     row_sum = factors[0]
                     for factor in factors[1:]:
                         row_sum = row_sum + factor
                 for a, rows in blocks:
                     total = None
-                    for j in range(particles):
-                        term = factors[j] * cols[j, a, rows, :]
+                    for j, factor in zip(others, factors):
+                        term = factor * cols[j, a, rows, :]
                         total = term if total is None else total + term
                     if model:
                         total = cols[i, a, rows, :] * row_sum - total
@@ -552,16 +576,24 @@
         own.start()
         return own
 
-    spread_out_rows(0, weight)
-    spread_own = mix(mcols, 0, mix_m, spread_out, 2, True)
+    for part in range(pairs // 128):
+        at = pl.ds(part * 128 // particles, 128 // particles)
+        KB[at] = rows_of(weight[part : part + 1, :]).reshape(128 // particles, particles, size_z)
+    spread_own = mix(mcols, mix_m, spread_out, 2, True)
 
     norm = sum_gather(norm_dom, "dom", 5)
     scale = 1.0 / jnp.sqrt(norm / float(total_x * total_y * size_z) + EPSILON)
-    spread_out_rows(1, weight * scale)
+    T[0] = rows_of(scale[0:1, :])[:particles]
     grad_own.wait()
     for copy in grad_moves:
         copy.wait()
-    drift_own = mix(gcols, 1, mix_g, drift_out, 3, False)
+    def divide(j, carry):
+        for a, rows in blocks:
+            gcols[j, a, rows, :] = gcols[j, a, rows, :] * T[0, pl.ds(j, 1), :]
+        return carry
+
+    lax.fori_loop(0, particles, divide, 0)
+    drift_own = mix(gcols, mix_g, drift_out, 3, False)
 
     spread_own.wait()
     drift_own.wait()
@@ -573,7 +605,7 @@
 
 def put_out(*refs):
     sem = refs[-1]
-    copies = [pltpu.make_async_copy(refs[k], refs[6 + k], sem.at[k]) for k in range(6)]
+    copies = [pltpu.make_async_copy(refs[k].at[p], refs[6 + k].at[p], sem.at[2 * k + p]) for k in range(6) for p in range(2)]
     for copy in copies:
         copy.start()
     for copy in copies:
@@ -593,19 +625,23 @@
     most = max(counts)
     hbm = pl.BlockSpec(memory_space=pltpu.HBM)
     vmem = pl.BlockSpec(memory_space=pltpu.VMEM)
-    smem = pl.BlockSpec(memory_space=pltpu.SMEM)
     dma = pltpu.SemaphoreType.DMA
     args = args[:9] + (jnp.transpose(args[9], (1, 0, 2)), args[10])
     results = pl.pallas_call(
         functools.partial(kernel, counts),
         out_shape=[pltpu.VMEM(whole, F32)] * 6,
-        in_specs=[hbm] * 6 + [smem, smem, vmem, vmem, smem],
+        in_specs=[hbm] * 11,
         out_specs=[vmem] * 6,
         scratch_shapes=[
+            pltpu.SMEM((parts,), jnp.int32),
+            pltpu.SMEM((parts, steps), F32),
+            pltpu.VMEM((parts, n_recv), jnp.int32),
+            pltpu.VMEM((steps, parts, n_recv), F32),
+            pltpu.SMEM((6,), jnp.int32),
             pltpu.VMEM((steps + 1, 2 * parts, pad_x, pad_y, size_z), F32),
             pltpu.VMEM(whole, F32),
             pltpu.VMEM((pad_x, pad_y, size_z), F32),
-            pltpu.VMEM((19, size_x, size_y, size_z), F32),
+            pltpu.VMEM((20, size_x, size_y, size_z), F32),
             pltpu.VMEM((size_x, size_y, size_z), F32),
             pltpu.VMEM(whole, F32),
             pltpu.VMEM((steps, parts, size_x * size_y, size_z), F32),
@@ -620,14 +656,14 @@
             pltpu.VMEM(cols, F32),
             pltpu.VMEM(cols, F32),
             pltpu.VMEM((particles, particles, size_z), F32),
-            pltpu.VMEM((2, particles, particles, size_z), F32),
+            pltpu.VMEM((particles, particles, size_z), F32),
             pltpu.VMEM((n_px, 8, size_z), F32),
             pltpu.VMEM((n_py, 8, size_z), F32),
             pltpu.VMEM((n_dom, 8, size_z), F32),
             pltpu.VMEM((n_px, 8, size_z), F32),
             pltpu.VMEM((n_py, 8, size_z), F32),
             pltpu.VMEM((n_dom, 8, size_z), F32),
-            dma((6,)),
+            dma((11,)),
             dma((1 + 2 * steps, 4)),
             dma((1 + 2 * steps, 4)),
             dma((4, n_dom)),
@@ -643,7 +679,7 @@
         out_shape=[jax.ShapeDtypeStruct(whole, F32)] * 6,
         in_specs=[vmem] * 6,
         out_specs=[hbm] * 6,
-        scratch_shapes=[dma((6,))],
+        scratch_shapes=[dma((12,))],
     )(*results)
 
 

time: 74.2 us -> 70.7 us (0.953)
  Pallas kernels: 73.4 us -> 69.7 us
    pallas_call x1, Pallas kernels: 71.7 us -> 67.9 us  [on_device(): pl.pallas_call(functools.partial(kernel, counts), out_shape=[pltpu.VMEM(w...]
where the time goes in v3:
time: 70.7 us; the launch traced here: 70.3 us
  Pallas kernels  69.7 us (99%)
    pallas_call x1, Pallas kernels, on_device(): pl.pallas_call(functools.partial(kernel, counts), out_shape=[pltpu.VMEM(w...  67.9 us
    pallas_call x1, Pallas kernels, on_device(): pl.pallas_call(put_out, out_shape=[jax.ShapeDtypeStruct(whole, F32)] * 6,...  1.76 us

profile of v3, /device:TPU:1, one launch (start us, length us, event | category | flops | bytes accessed | tf_op | source)
XLA Modules:
  0.0 70.3 jit_solution(4341422984936989634)
XLA Ops:
  0.6 67.9 %shard_map.154 = (f32[2,16,32,128]{3,2,1,0:T(8,128)S(1)}, f32[2,16,32,128]{3,2,1,0:T(8,128)S(1)}, f32[2,16,32,128]{3,2,1,0:T(8,128)S(1)}, f32[2,16,32,128]{3,2,1...) custom-call(f32[2,16,32,128]{3,2,1,0:T(8,128)} %vel_in.1, f32[16,32,128]{2,1,0:T(8,128)} %buoy_in.1, ...), custom_call_target="tpu_custom_call" | custom-call | tf_op jit(solution)/shard_map/pallas_call | solution.py:630
  68.6 1.8 %shard_map.155 = (f32[2,16,32,128]{3,2,1,0:T(8,128)}, f32[2,16,32,128]{3,2,1,0:T(8,128)}, f32[2,16,32,128]{3,2,1,0:T(8,128)}, f32[2,16,32,128]{3,2,1,0:T(8,128)}...) custom-call(f32[2,16,32,128]{3,2,1,0:T(8,128)S(1)} %get-tuple-element.12.refs_0_, ...), custom_call_target="tpu_custom_call" | custom-call | tf_op jit(solution)/shard_map/pallas_call | solution.py:677

commit v4 on v3

--- a/solution.py
+++ b/solution.py
@@ -89,11 +89,11 @@
     mix_g,
     T,
     KB,
-    gram_px,
-    gram_py,
+    gram_core,
+    gram_plane,
     gram_dom,
-    norm_px,
-    norm_py,
+    norm_core,
+    norm_plane,
     norm_dom,
     load_sem,
     halo_send,
@@ -121,9 +121,10 @@
         return lax.rem(coord[axis] + k, count[axis])
 
     barrier = pltpu.get_barrier_semaphore()
-    for axis in ("px", "py", "dom"):
-        for k in range(1, count[axis]):
-            pl.semaphore_signal(barrier, inc=1, device_id={axis: peer(axis, k)}, device_id_type=MESH)
+    met = [{axis: peer(axis, k)} for axis in ("px", "py", "dom") for k in range(1, count[axis])]
+    met += [{"px": peer("px", 2 * c), "py": peer("py", k)} for c in range(1, n_px // 2) for k in range(1, n_py)]
+    for device in met:
+        pl.semaphore_signal(barrier, inc=1, device_id=device, device_id_type=MESH)
 
     loads = [
         pltpu.make_async_copy(vel_in, vel, load_sem.at[0]),
@@ -142,8 +143,8 @@
     )
     for at, (src, dst) in enumerate(small):
         loads.append(pltpu.make_async_copy(src, dst, load_sem.at[6 + at]))
-    for copy in loads:
-        copy.start()
+    for at in (1, 2, 3, 0, *range(4, len(loads))):
+        loads[at].start()
 
     zero_rows = jnp.zeros((8, size_z), F32)
     zero_plane = jnp.zeros((size_y, size_z), F32)
@@ -170,17 +171,17 @@
     pl.when(py == 0)(lambda: zero_strip(0))
     pl.when(py == n_py - 1)(lambda: zero_strip(TOP + size_y))
 
-    def halo_copies(ref, lead, group):
+    def halo_copies(ref, lead, group, deep=EDGE):
         def at(x, y):
             return ref.at[lead + (x, y)]
 
         x_all, y_all = cells
         last_x, last_y = EDGE + size_x, TOP + size_y
         moves = (
-            ("px", 1, at(pl.ds(last_x - EDGE, EDGE), y_all), at(pl.ds(0, EDGE), y_all)),
-            ("px", -1, at(pl.ds(EDGE, EDGE), y_all), at(pl.ds(last_x, EDGE), y_all)),
-            ("py", 1, at(x_all, pl.ds(last_y - EDGE, EDGE)), at(x_all, pl.ds(TOP - EDGE, EDGE))),
-            ("py", -1, at(x_all, pl.ds(TOP, EDGE)), at(x_all, pl.ds(last_y, EDGE))),
+            ("px", 1, at(pl.ds(last_x - deep, deep), y_all), at(pl.ds(EDGE - deep, deep), y_all)),
+            ("px", -1, at(pl.ds(EDGE, deep), y_all), at(pl.ds(last_x, deep), y_all)),
+            ("py", 1, at(x_all, pl.ds(last_y - deep, deep)), at(x_all, pl.ds(TOP - deep, deep))),
+            ("py", -1, at(x_all, pl.ds(TOP, deep)), at(x_all, pl.ds(last_y, deep))),
         )
         copies = []
         for way, (axis, k, src, dst) in enumerate(moves):
@@ -198,78 +199,97 @@
         can_recv = (px > 0, px < n_px - 1, py > 0, py < n_py - 1)
         return copies, can_send, can_recv
 
-    def send_halo(halo):
+    def send_halo(halo, ways=(2, 3, 0, 1)):
         copies, can_send, _ = halo
-        for way in (2, 3, 0, 1):
+        for way in ways:
             pl.when(can_send[way])(copies[way].start)
 
-    def wait_halo(halo):
+    x_ways, y_ways = (0, 1), (2, 3)
+
+    def wait_halo(halo, ways=(0, 1, 2, 3)):
         copies, can_send, can_recv = halo
-        for way in range(4):
+        for way in ways:
             pl.when(can_send[way])(copies[way].wait_send)
             pl.when(can_recv[way])(copies[way].wait_recv)
 
-    halo_b = halo_copies(bpad, (), 0)
+    halo_b = halo_copies(bpad, (), 0, EDGE - 1)
     halo_w = {
         (state, kind): halo_copies(S, (state, pl.ds(kind * parts, parts)), 2 * state - 1 + kind)
         for state in range(1, 1 + steps)
         for kind in range(2)
     }
 
-    def column_copies(values, cols, lane):
+    far_first = sorted(range(1, n_dom), key=lambda k: abs(n_dom - 2 * k))
+
+    def column_copies(values, cols, lane, rows=pl.ds(0, size_y)):
         return [
             pltpu.make_async_remote_copy(
-                values.at[:, pl.ds(peer("dom", k) * share, share)],
-                cols.at[pl.ds(dom * parts, parts)],
+                values.at[:, pl.ds(peer("dom", k) * share, share), rows],
+                cols.at[pl.ds(dom * parts, parts), :, rows],
                 col_send.at[lane, k],
                 col_recv.at[lane, k],
                 device_id={"dom": peer("dom", k)},
                 device_id_type=MESH,
             )
-            for k in range(1, n_dom)
+            for k in far_first
         ]
 
-    def own_column(values, cols, lane):
+    def own_column(values, cols, lane, rows=pl.ds(0, size_y)):
         return pltpu.make_async_copy(
-            values.at[:, pl.ds(dom * share, share)], cols.at[pl.ds(dom * parts, parts)], col_send.at[lane, 0]
+            values.at[:, pl.ds(dom * share, share), rows],
+            cols.at[pl.ds(dom * parts, parts), :, rows],
+            col_send.at[lane, 0],
         )
 
-    slots = []
-    for _ in range(2):
-        for axis in ("px", "py", "dom"):
-            slots.append(axis)
-
-    def sum_copies(buffer, axis, slot):
+    def group_of(name):
+        if name == "dom":
+            return dom, n_dom, lambda k: {"dom": peer("dom", k)}
+        if name == "core":
+            return lax.rem(px, 2), 2, lambda k: {"px": px + 1 - 2 * lax.rem(px, 2)}
+        size = n_px // 2 * n_py
+        index = lax.div(px, 2) * n_py + py
+
+        def device(k):
+            at = lax.rem(index + k, size)
+            return {"px": lax.div(at, n_py) * 2 + lax.rem(px, 2), "py": lax.rem(at, n_py)}
+
+        return index, size, device
+
+    def sum_copies(buffer, name, slot):
+        index, size, device = group_of(name)
         return [
             pltpu.make_async_remote_copy(
-                buffer.at[coord[axis]],
-                buffer.at[coord[axis]],
+                buffer.at[index, pl.ds(0, 2)],
+                buffer.at[index, pl.ds(0, 2)],
                 sum_send.at[slot, k],
                 sum_recv.at[slot, k],
-                device_id={axis: peer(axis, k)},
+                device_id=device(k),
                 device_id_type=MESH,
             )
-            for k in range(1, count[axis])
+            for k in range(1, size)
         ]
 
-    def sum_send_off(buffer, axis, slot, value):
-        buffer[coord[axis]] = value
-        for copy in sum_copies(buffer, axis, slot):
+    def sum_send_off(buffer, name, slot, value):
+        buffer[group_of(name)[0], pl.ds(0, 2), :] = value
+        for copy in sum_copies(buffer, name, slot):
             copy.start()
 
-    def sum_gather(buffer, axis, slot):
-        for copy in sum_copies(buffer, axis, slot):
+    def sum_gather(buffer, name, slot):
+        for copy in sum_copies(buffer, name, slot):
             copy.wait()
-        value = buffer[0]
-        for k in range(1, count[axis]):
-            value = value + buffer[k]
+        value = buffer[0, pl.ds(0, 2), :]
+        for k in range(1, group_of(name)[1]):
+            value = value + buffer[k, pl.ds(0, 2), :]
         return value
 
-    def pre_step(step, kind):
+    every = tuple(range(tiles))
+    inner, outer = every[1:-1], (0, tiles - 1)
+
+    def pre_plane(step, kind, chosen):
         now, before = step + 1, step
 
         def plane(x, carry):
-            for t in range(tiles):
+            for t in chosen:
                 rows, wide = pl.ds(8 * t, 8), pl.ds(TOP + 8 * t, 8)
                 weights = [C[k, x, rows, :] for k in (0, 13, 14, 15, 16, 17, 18)]
                 fade = damp[x, rows, :]
@@ -293,15 +313,15 @@
                         grad[p, x, rows, :] = part
             return carry
 
-        lax.fori_loop(0, size_x, plane, 0, unroll=2)
-
-    def post_step(step, kind):
+        return plane
+
+    def post_plane(step, kind, chosen):
         now, before, later = step + 1, step, step + 2
         last = step == steps - 1
 
         def plane(x, carry):
             sums = list(carry)
-            for t in range(tiles):
+            for t in chosen:
                 rows, wide = pl.ds(8 * t, 8), pl.ds(TOP + 8 * t, 8)
                 weights = [C[1 + k, x, rows, :] for k in range(12)] + [C[19, x, rows, :]]
                 for p in range(parts):
@@ -327,24 +347,37 @@
                         grad[p, x, rows, :] = part
             return tuple(sums)
 
-        start = tuple(jnp.zeros((8, size_z), F32) for _ in range(parts)) if kind == 0 and last else ()
-        return lax.fori_loop(0, size_x, plane, start, unroll=2)
+        return plane
+
+    def pre_step(step, kind, chosen=every):
+        lax.fori_loop(0, size_x, pre_plane(step, kind, chosen), 0, unroll=2 * tiles // len(chosen))
+
+    def post_step(step, kind, chosen=every, start=()):
+        return lax.fori_loop(0, size_x, post_plane(step, kind, chosen), start, unroll=2 * tiles // len(chosen))
+
+    def post_and_pre(post, pre):
+        after, ahead = post_plane(*post, every), pre_plane(*pre, every)
+
+        def plane(x, carry):
+            after(x, ())
+            ahead(x, 0)
+            return carry
+
+        lax.fori_loop(0, size_x, plane, 0, unroll=2)
 
     results = ((fb_out, fa_out), (ab_out, aa_out))
 
-    for copy in loads[:4]:
-        copy.wait()
-    pl.semaphore_wait(barrier, (n_px - 1) + (n_py - 1) + (n_dom - 1))
-    send_halo(halo_b)
-    send_halo(halo_w[1, 0])
-    send_halo(halo_w[1, 1])
-    model_moves = column_copies(vel, mcols, 0)
+    pl.semaphore_wait(barrier, len(met))
+    model_moves = [*column_copies(vel_in, mcols, 0), own_column(vel_in, mcols, 0)]
     for copy in model_moves:
         copy.start()
-    model_own = own_column(vel, mcols, 0)
-    model_own.start()
-
-    for copy in loads[6:]:
+    loads[1].wait()
+    send_halo(halo_b)
+    loads[2].wait()
+    send_halo(halo_w[1, 0])
+    loads[3].wait()
+    send_halo(halo_w[1, 1])
+    for copy in [loads[0], *loads[6:]]:
         copy.wait()
 
     widths = [sponge[k].astype(F32) for k in range(6)]
@@ -376,41 +409,51 @@
     n_recv = receivers.shape[1]
     row16 = lax.broadcasted_iota(jnp.int32, (16, n_recv), 0)
 
-    def inject(p):
-        index = receivers[pl.ds(p, 1), :]
+    def recv_index(p):
+        return receivers[pl.ds(p, 1), :]
+
+    def mark_planes(p):
+        index = recv_index(p)
         local_x = (index >> (z_bits + y_bits)) - base_x
         local_y = ((index >> z_bits) & (total_y - 1)) - base_y
         inside = (local_x >= 0) & (local_x < size_x) & (local_y >= 0) & (local_y < size_y)
         at_plane = jnp.where(inside, local_x * size_y + local_y, -1) - row16
-        depth = (index & (size_z - 1)) - row16
+
+        def planes(m, carry):
+            hot[p, pl.ds(pl.multiple_of(m * 16, 16), 16), :] = jnp.where(at_plane == m * 16, 1.0, 0.0).astype(BF16)
+            return carry
+
+        lax.fori_loop(0, size_x * size_y // 16, planes, 0, unroll=2)
+
+    def inject(p, chosen_steps):
+        depth = (recv_index(p) & (size_z - 1)) - row16
         amounts = []
-        for s in range(steps):
+        for s in chosen_steps:
             amount = STEP_SQ * misfit[s, pl.ds(p, 1), :]
             high = amount.astype(BF16).astype(F32)
             amounts += [high, amount - high]
 
         def depths(m, carry):
             hit = depth == m * 16
+            at = pl.ds(pl.multiple_of(m * 16, 16), 16)
             for k, amount in enumerate(amounts):
-                b_parts[k, pl.ds(pl.multiple_of(m * 16, 16), 16), :] = jnp.where(hit, amount, 0.0).astype(BF16)
+                b_parts[p, k, at, :] = jnp.where(hit, amount, 0.0).astype(BF16)
             return carry
 
         lax.fori_loop(0, size_z // 16, depths, 0)
-
-        def planes(m, carry):
-            hot[pl.ds(pl.multiple_of(m * 16, 16), 16), :] = jnp.where(at_plane == m * 16, 1.0, 0.0).astype(BF16)
-            return carry
-
-        lax.fori_loop(0, size_x * size_y // 16, planes, 0, unroll=2)
-        for s in range(steps):
-            both = lax.dot_general(
-                hot[...],
-                b_parts[pl.ds(2 * s, 2)].reshape(2 * size_z, n_recv),
-                NT,
-                preferred_element_type=F32,
-            )
-            inj[s, p] = both[:, :size_z] + both[:, size_z:]
-
+        both = lax.dot_general(
+            hot[p],
+            b_parts[p, pl.ds(0, len(amounts))].reshape(len(amounts) * size_z, n_recv),
+            NT,
+            preferred_element_type=F32,
+        )
+        for k, s in enumerate(chosen_steps):
+            first = 2 * k * size_z
+            inj[s, p] = both[:, first : first + size_z] + both[:, first + size_z : first + 2 * size_z]
+
+    def inject_all(*chosen_steps):
+        for p in range(parts):
+            inject(p, chosen_steps)
 
     def face_weights(around, scale):
         return axis_coefs([scale * (around[k] + around[k + 1]) for k in (-2, -1, 0, 1)])
@@ -443,30 +486,31 @@
         return carry
 
     within = {k: (lane8 + k >= 0) & (lane8 + k < size_z) for k in SHIFTS}
-    lax.fori_loop(0, size_x, stencil_z, 0)
+    lax.fori_loop(0, size_x, stencil_z, 0, unroll=4)
     for copy in loads[4:6]:
         copy.wait()
     pre_step(0, 0)
-    inject(0)
+    for p in range(parts):
+        mark_planes(p)
+    inject_all(0, 1)
     wait_halo(halo_b)
     lax.fori_loop(0, size_x, stencil_xy, 0)
 
-    wait_halo(halo_w[1, 0])
-    post_step(0, 0)
+    wait_halo(halo_w[1, 0], x_ways)
+    post_step(0, 0, inner)
+    wait_halo(halo_w[1, 0], y_ways)
+    post_step(0, 0, outer)
     send_halo(halo_w[2, 0])
-    for p in range(1, parts):
-        inject(p)
     pre_step(0, 1)
     wait_halo(halo_w[1, 1])
-    post_step(0, 1)
-    send_halo(halo_w[2, 1])
-    pre_step(1, 0)
-    wait_halo(halo_w[2, 0])
-    post_step(1, 0)
-    send_halo(halo_w[3, 0])
-    pre_step(2, 0)
-
-    model_own.wait()
+    post_and_pre((0, 1), (1, 0))
+    send_halo(halo_w[2, 1], x_ways + y_ways)
+    pre_step(1, 1)
+    wait_halo(halo_w[2, 0], x_ways)
+    post_step(1, 0, inner)
+    wait_halo(halo_w[2, 0], y_ways)
+    post_step(1, 0, outer)
+    send_halo(halo_w[3, 0], x_ways)
     for copy in model_moves:
         copy.wait()
     blocks = [(a, pl.ds(8 * t, 8)) for a in range(share) for t in range(tiles)]
@@ -494,40 +538,46 @@
         precision=HIGHEST,
         preferred_element_type=F32,
     )
-    gram = jnp.where(row8 == 0, lane_sums[:, :128], lane_sums[:, 128:])
+    gram = jnp.where(row8 == 0, lane_sums[:, :128], lane_sums[:, 128:])[:2]
     sum_send_off(gram_dom, "dom", 2, gram)
-    pre_step(1, 1)
-    wait_halo(halo_w[2, 1])
-    post_step(1, 1)
-    send_halo(halo_w[3, 1])
-
-    wait_halo(halo_w[3, 0])
-    grad_sums = post_step(2, 0)
-    grad_moves = column_copies(grad, gcols, 1)
-    for copy in grad_moves:
-        copy.start()
-    grad_own = own_column(grad, gcols, 1)
-    grad_own.start()
-    norm = jnp.zeros((8, size_z), F32)
+
+    send_halo(halo_w[3, 0], y_ways)
+    pre_step(2, 0, inner)
+    wait_halo(halo_w[2, 1], x_ways)
+    post_step(1, 1, inner)
+
+    wait_halo(halo_w[3, 0], x_ways)
+    grad_sums = post_step(2, 0, inner, tuple(jnp.zeros((8, size_z), F32) for _ in range(parts)))
+    grad_moves = []
+
+    def send_grad(lane, rows):
+        for copy in [*column_copies(grad, gcols, lane, rows), own_column(grad, gcols, lane, rows)]:
+            copy.start()
+            grad_moves.append(copy)
+
+    send_grad(1, pl.ds(8, size_y - 16))
+    pre_step(2, 0, outer)
+    wait_halo(halo_w[2, 1], y_ways)
+    post_step(1, 1, outer)
+    gram = sum_gather(gram_dom, "dom", 2)
+    sum_send_off(gram_core, "core", 0, gram)
+    wait_halo(halo_w[3, 0], y_ways)
+    grad_sums = post_step(2, 0, outer, grad_sums)
+    send_grad(4, pl.ds(0, 8))
+    send_grad(5, pl.ds(size_y - 8, 8))
+    lane2 = lax.broadcasted_iota(jnp.int32, (2, size_z), 1)
+    norm = jnp.zeros((2, size_z), F32)
     for p in range(parts):
-        norm = jnp.where(lane8 % particles == dom * parts + p, jnp.sum(grad_sums[p]), norm)
-    sum_send_off(norm_px, "px", 3, norm)
-    gram = sum_gather(gram_dom, "dom", 2)
-    sum_send_off(gram_px, "px", 0, gram)
-    norm = sum_gather(norm_px, "px", 3)
-    sum_send_off(norm_py, "py", 4, norm)
-    gram = sum_gather(gram_px, "px", 0)
-    sum_send_off(gram_py, "py", 1, gram)
-
-    pre_step(2, 1)
-    wait_halo(halo_w[3, 1])
-    post_step(2, 1)
-    norm = sum_gather(norm_py, "py", 4)
-    sum_send_off(norm_dom, "dom", 5, norm)
-    gram = sum_gather(gram_py, "py", 1)
-
-    twice = jnp.where(lane8 % particles == half, 1.0, 2.0)
-    width = jnp.sum(jnp.where(row8 < 2, gram * twice, 0.0)) / (particles * (particles - 1)) + EPSILON
+        norm = jnp.where(lane2 % particles == dom * parts + p, jnp.sum(grad_sums[p]), norm)
+    sum_send_off(norm_core, "core", 3, norm)
+    gram = sum_gather(gram_core, "core", 0)
+    sum_send_off(gram_plane, "plane", 1, gram)
+    norm = sum_gather(norm_core, "core", 3)
+    sum_send_off(norm_plane, "plane", 4, norm)
+    gram = sum_gather(gram_plane, "plane", 1)
+
+    twice = jnp.where(lane2 % particles == half, 1.0, 2.0)
+    width = jnp.sum(gram * twice) / (particles * (particles - 1)) + EPSILON
     weight = jnp.exp(-gram / width)
     square = lax.broadcasted_iota(jnp.int32, (128, 128), 0) == lax.broadcasted_iota(jnp.int32, (128, 128), 1)
 
@@ -547,7 +597,9 @@
         )
 
     def mix(cols, mixed, out, sem_lane, model):
-        def one(k, carry):
+        def one(n, carry):
+            far = lax.div(n + 1, 2)
+            k = n_dom // 2 + jnp.where(lax.rem(n, 2) == 1, -far, far)
             target = lax.rem(dom + k, n_dom)
             for p in range(parts):
                 i = target * parts + p
@@ -566,10 +618,10 @@
                     if model:
                         total = cols[i, a, rows, :] * row_sum - total
                     mixed[i, a, rows, :] = total
-            pl.when(k < n_dom)(lambda: back_copy(mixed, out, sem_lane, lax.rem(k, n_dom), target).start())
+            pl.when(k > 0)(lambda: back_copy(mixed, out, sem_lane, k, target).start())
             return carry
 
-        lax.fori_loop(1, n_dom + 1, one, 0)
+        lax.fori_loop(0, n_dom, one, 0)
         own = pltpu.make_async_copy(
             mixed.at[pl.ds(dom * parts, parts)], out.at[:, pl.ds(dom * share, share)], col_send.at[sem_lane, 0]
         )
@@ -579,12 +631,17 @@
     for part in range(pairs // 128):
         at = pl.ds(part * 128 // particles, 128 // particles)
         KB[at] = rows_of(weight[part : part + 1, :]).reshape(128 // particles, particles, size_z)
+    norm = sum_gather(norm_plane, "plane", 4)
+    sum_send_off(norm_dom, "dom", 5, norm)
+    send_halo(halo_w[3, 1])
     spread_own = mix(mcols, mix_m, spread_out, 2, True)
+
+    inject_all(2)
+    pre_step(2, 1)
 
     norm = sum_gather(norm_dom, "dom", 5)
     scale = 1.0 / jnp.sqrt(norm / float(total_x * total_y * size_z) + EPSILON)
     T[0] = rows_of(scale[0:1, :])[:particles]
-    grad_own.wait()
     for copy in grad_moves:
         copy.wait()
     def divide(j, carry):
@@ -595,6 +652,8 @@
     lax.fori_loop(0, particles, divide, 0)
     drift_own = mix(gcols, mix_g, drift_out, 3, False)
 
+    wait_halo(halo_w[3, 1])
+    post_step(2, 1)
     spread_own.wait()
     drift_own.wait()
     for k in range(1, n_dom):
@@ -622,7 +681,7 @@
     pad_x, pad_y = size_x + 2 * EDGE, size_y + 2 * TOP
     whole = (parts, size_x, size_y, size_z)
     cols = (particles, share, size_y, size_z)
-    most = max(counts)
+    most = max(n_dom, n_px // 2 * n_py)
     hbm = pl.BlockSpec(memory_space=pltpu.HBM)
     vmem = pl.BlockSpec(memory_space=pltpu.VMEM)
     dma = pltpu.SemaphoreType.DMA
@@ -645,8 +704,8 @@
             pltpu.VMEM((size_x, size_y, size_z), F32),
             pltpu.VMEM(whole, F32),
             pltpu.VMEM((steps, parts, size_x * size_y, size_z), F32),
-            pltpu.VMEM((2 * steps, size_z, n_recv), BF16),
-            pltpu.VMEM((size_x * size_y, n_recv), BF16),
+            pltpu.VMEM((parts, 2 * steps, size_z, n_recv), BF16),
+            pltpu.VMEM((parts, size_x * size_y, n_recv), BF16),
             pltpu.VMEM(whole, F32),
             pltpu.VMEM(whole, F32),
             pltpu.VMEM((2,) + whole, F32),
@@ -657,17 +716,17 @@
             pltpu.VMEM(cols, F32),
             pltpu.VMEM((particles, particles, size_z), F32),
             pltpu.VMEM((particles, particles, size_z), F32),
-            pltpu.VMEM((n_px, 8, size_z), F32),
-            pltpu.VMEM((n_py, 8, size_z), F32),
+            pltpu.VMEM((2, 8, size_z), F32),
+            pltpu.VMEM((n_px // 2 * n_py, 8, size_z), F32),
             pltpu.VMEM((n_dom, 8, size_z), F32),
-            pltpu.VMEM((n_px, 8, size_z), F32),
-            pltpu.VMEM((n_py, 8, size_z), F32),
+            pltpu.VMEM((2, 8, size_z), F32),
+            pltpu.VMEM((n_px // 2 * n_py, 8, size_z), F32),
             pltpu.VMEM((n_dom, 8, size_z), F32),
             dma((11,)),
             dma((1 + 2 * steps, 4)),
             dma((1 + 2 * steps, 4)),
-            dma((4, n_dom)),
-            dma((4, n_dom)),
+            dma((6, n_dom)),
+            dma((6, n_dom)),
             dma((6, most)),
             dma((6, most)),
         ],

time: 70.7 us -> 69 us (0.976)
  Pallas kernels: 69.7 us -> 68.3 us
    pallas_call x1, Pallas kernels: 67.9 us -> 66.5 us  [on_device(): pl.pallas_call(functools.partial(kernel, counts), out_shape=[pltpu.VMEM(w...]
where the time goes in v4:
time: 69 us; the launch traced here: 68.9 us
  Pallas kernels  68.3 us (99%)
    pallas_call x1, Pallas kernels, on_device(): pl.pallas_call(functools.partial(kernel, counts), out_shape=[pltpu.VMEM(w...  66.5 us
    pallas_call x1, Pallas kernels, on_device(): pl.pallas_call(put_out, out_shape=[jax.ShapeDtypeStruct(whole, F32)] * 6,...  1.76 us

profile of v4, /device:TPU:1, one launch (start us, length us, event | category | flops | bytes accessed | tf_op | source)
XLA Modules:
  0.0 68.9 jit_solution(3981098306893719682)
XLA Ops:
  0.6 66.5 %shard_map.154 = (f32[2,16,32,128]{3,2,1,0:T(8,128)S(1)}, f32[2,16,32,128]{3,2,1,0:T(8,128)S(1)}, f32[2,16,32,128]{3,2,1,0:T(8,128)S(1)}, f32[2,16,32,128]{3,2,1...) custom-call(f32[2,16,32,128]{3,2,1,0:T(8,128)} %vel_in.1, f32[16,32,128]{2,1,0:T(8,128)} %buoy_in.1, ...), custom_call_target="tpu_custom_call" | custom-call | tf_op jit(solution)/shard_map/pallas_call | solution.py:689
  67.2 1.8 %shard_map.155 = (f32[2,16,32,128]{3,2,1,0:T(8,128)}, f32[2,16,32,128]{3,2,1,0:T(8,128)}, f32[2,16,32,128]{3,2,1,0:T(8,128)}, f32[2,16,32,128]{3,2,1,0:T(8,128)}...) custom-call(f32[2,16,32,128]{3,2,1,0:T(8,128)S(1)} %get-tuple-element.12.refs_0_, ...), custom_call_target="tpu_custom_call" | custom-call | tf_op jit(solution)/shard_map/pallas_call | solution.py:736

commit v5 on v4

--- a/solution.py
+++ b/solution.py
@@ -352,8 +352,10 @@
     def pre_step(step, kind, chosen=every):
         lax.fori_loop(0, size_x, pre_plane(step, kind, chosen), 0, unroll=2 * tiles // len(chosen))
 
-    def post_step(step, kind, chosen=every, start=()):
-        return lax.fori_loop(0, size_x, post_plane(step, kind, chosen), start, unroll=2 * tiles // len(chosen))
+    def post_step(step, kind, chosen=every, carry=(), spans=((0, size_x),)):
+        for first, end in spans:
+            carry = lax.fori_loop(first, end, post_plane(step, kind, chosen), carry, unroll=2 * tiles // len(chosen))
+        return carry
 
     def post_and_pre(post, pre):
         after, ahead = post_plane(*post, every), pre_plane(*pre, every)
@@ -543,28 +545,41 @@
 
     send_halo(halo_w[3, 0], y_ways)
     pre_step(2, 0, inner)
+    low = -(-EDGE // share) * share
+    middle, ends = ((low, size_x - low),), ((0, low), (size_x - low, size_x))
+    post_step(1, 1, inner, (), middle)
+    grad_sums = post_step(2, 0, inner, tuple(jnp.zeros((8, size_z), F32) for _ in range(parts)), middle)
+    grad_moves = []
+
+    def grad_copies(lane, rows):
+        copies = column_copies(grad, gcols, lane, rows)
+        grad_moves.extend([*copies, own_column(grad, gcols, lane, rows)])
+        return copies, grad_moves[-1]
+
+    half_moves, half_own = grad_copies(1, pl.ds(8, size_y - 16))
+    mid_owner = []
+    for copy, k in zip(half_moves, far_first):
+        target = peer("dom", k)
+        mid_owner.append((target >= low // share) & (target < n_dom - low // share))
+        pl.when(mid_owner[-1])(copy.start)
     wait_halo(halo_w[2, 1], x_ways)
-    post_step(1, 1, inner)
-
+    post_step(1, 1, inner, (), ends)
     wait_halo(halo_w[3, 0], x_ways)
-    grad_sums = post_step(2, 0, inner, tuple(jnp.zeros((8, size_z), F32) for _ in range(parts)))
-    grad_moves = []
-
-    def send_grad(lane, rows):
-        for copy in [*column_copies(grad, gcols, lane, rows), own_column(grad, gcols, lane, rows)]:
-            copy.start()
-            grad_moves.append(copy)
-
-    send_grad(1, pl.ds(8, size_y - 16))
+    grad_sums = post_step(2, 0, inner, grad_sums, ends)
+    for copy, owner in zip(half_moves, mid_owner):
+        pl.when(jnp.logical_not(owner))(copy.start)
+    half_own.start()
+    gram = sum_gather(gram_dom, "dom", 2)
+    sum_send_off(gram_core, "core", 0, gram)
     pre_step(2, 0, outer)
     wait_halo(halo_w[2, 1], y_ways)
     post_step(1, 1, outer)
-    gram = sum_gather(gram_dom, "dom", 2)
-    sum_send_off(gram_core, "core", 0, gram)
     wait_halo(halo_w[3, 0], y_ways)
     grad_sums = post_step(2, 0, outer, grad_sums)
-    send_grad(4, pl.ds(0, 8))
-    send_grad(5, pl.ds(size_y - 8, 8))
+    for lane, first in ((4, 0), (5, size_y - 8)):
+        copies, own = grad_copies(lane, pl.ds(first, 8))
+        for copy in [*copies, own]:
+            copy.start()
     lane2 = lax.broadcasted_iota(jnp.int32, (2, size_z), 1)
     norm = jnp.zeros((2, size_z), F32)
     for p in range(parts):

time: 69 us -> 68.7 us (level)
  no operation moved by 1% of the time
where the time goes in v5:
time: 68.7 us; the launch traced here: 68.6 us
  Pallas kernels  67.9 us (99%)
    pallas_call x1, Pallas kernels, on_device(): pl.pallas_call(functools.partial(kernel, counts), out_shape=[pltpu.VMEM(w...  66.2 us
    pallas_call x1, Pallas kernels, on_device(): pl.pallas_call(put_out, out_shape=[jax.ShapeDtypeStruct(whole, F32)] * 6,...  1.76 us

profile of v5, /device:TPU:1, one launch (start us, length us, event | category | flops | bytes accessed | tf_op | source)
XLA Modules:
  0.0 68.6 jit_solution(5955350648285094330)
XLA Ops:
  0.6 66.2 %shard_map.154 = (f32[2,16,32,128]{3,2,1,0:T(8,128)S(1)}, f32[2,16,32,128]{3,2,1,0:T(8,128)S(1)}, f32[2,16,32,128]{3,2,1,0:T(8,128)S(1)}, f32[2,16,32,128]{3,2,1...) custom-call(f32[2,16,32,128]{3,2,1,0:T(8,128)} %vel_in.1, f32[16,32,128]{2,1,0:T(8,128)} %buoy_in.1, ...), custom_call_target="tpu_custom_call" | custom-call | tf_op jit(solution)/shard_map/pallas_call | solution.py:704
  66.8 1.8 %shard_map.155 = (f32[2,16,32,128]{3,2,1,0:T(8,128)}, f32[2,16,32,128]{3,2,1,0:T(8,128)}, f32[2,16,32,128]{3,2,1,0:T(8,128)}, f32[2,16,32,128]{3,2,1,0:T(8,128)}...) custom-call(f32[2,16,32,128]{3,2,1,0:T(8,128)S(1)} %get-tuple-element.12.refs_0_, ...), custom_call_target="tpu_custom_call" | custom-call | tf_op jit(solution)/shard_map/pallas_call | solution.py:751
